TPU v7x, 32 devices: a whole 2x2x4 slice. The times are simulated.
32 devices in a mesh: seq: 16 (over z, x, core), head: 2 (over y).
Axes of the slice: x: 2, y: 2, z: 4, core: 2. Of those that a mesh axis runs over, the one named last changes fastest.
Arguments:
- queries: bfloat16 [16384, 4096], P('seq', 'head'), may hold values from -90 to 90
- keys: bfloat16 [16384, 4096], P('seq', 'head'), may hold values from -50 to 50
- values: bfloat16 [16384, 4096], P('seq', 'head'), may hold values from -6 to 6
- cluster_ids: int32 [16384, 32], P('seq', 'head'), may hold values from 0 to 255, as said below
- out_weight: bfloat16 [4096, 4096], P('head', 'seq'), may hold values from -2.390625 to 2.390625
Outputs:
- mixed: bfloat16 [16384, 4096], P('seq', 'head')
Inputs may be any that keep to these rules, and one draw needn't show every extreme that they name: `cluster_ids`: in every head each of the 256 clusters holds at least one token.
All inputs are finite; a program needn't handle non-finite values.
Results may differ from a plain program's by a relative error of at most 0.01.
Values may be sent and summed in bfloat16 or wider, within the bound.
A program may use at most 128 MiB of HBM per device.

v0:
```python
import jax
import jax.numpy as jnp
from jax import lax
from jax.sharding import PartitionSpec as P

HDIM = 128
CLUSTERS = 256


def local(queries, keys, values, cluster_ids, out_weight):
    token_rows = queries.shape[0]
    head_count = queries.shape[1] // HDIM
    query_three = queries.reshape(token_rows, head_count, HDIM)
    key_three = keys.reshape(token_rows, head_count, HDIM)
    value_three = values.reshape(token_rows, head_count, HDIM)
    labels = jnp.arange(CLUSTERS, dtype=jnp.int32)
    wide_rows = lax.all_gather(out_weight, "seq", axis=1, tiled=True)
    column_weight = lax.all_to_all(wide_rows, "head", split_axis=1, concat_axis=0, tiled=True)
    labels_every = lax.all_gather(cluster_ids, "head", axis=1, tiled=True)
    member = (cluster_ids[:, :, None] == labels[None, None, :]).astype(jnp.bfloat16)
    totals = jnp.einsum("thc,thd->hcd", member, query_three, preferred_element_type=jnp.float32)
    counts = jnp.sum(member, axis=0, dtype=jnp.float32)
    all_totals, all_counts = lax.psum((totals, counts), "seq")
    centre = (all_totals / all_counts[:, :, None]).astype(jnp.bfloat16)
    scores = jnp.einsum("hcd,thd->hct", centre, key_three, preferred_element_type=jnp.float32)
    scores = scores * (1.0 / HDIM**0.5)
    block_peak = jnp.max(scores, axis=2)
    weights = jnp.exp(scores - block_peak[:, :, None]).astype(jnp.bfloat16)
    block_mass = jnp.sum(weights, axis=2, dtype=jnp.float32)
    block_output = jnp.einsum(
        "hct,thd->hcd", weights, value_three, preferred_element_type=jnp.float32
    )
    global_peak = lax.pmax(block_peak, "seq")
    factor = jnp.exp(block_peak - global_peak)
    mass_sum, output_sum = lax.psum((block_mass * factor, block_output * factor[:, :, None]), "seq")
    centroid_out = (output_sum / mass_sum[:, :, None]).astype(jnp.bfloat16)
    centre_every = lax.all_gather(centroid_out, "head", axis=0, tiled=True)
    member_every = (labels_every[:, :, None] == labels[None, None, :]).astype(jnp.bfloat16)
    attended_all = jnp.einsum(
        "thc,hcd->thd", member_every, centre_every, preferred_element_type=jnp.float32
    )
    attended_all = attended_all.astype(jnp.bfloat16).reshape(token_rows, -1)
    group_count = lax.axis_size("head")
    group_rows = attended_all.shape[1] // group_count
    summed = jnp.zeros((token_rows, column_weight.shape[1]), jnp.float32)
    for group in range(group_count):
        term = jnp.dot(
            attended_all[:, group * group_rows : (group + 1) * group_rows],
            column_weight[group * group_rows : (group + 1) * group_rows, :],
            preferred_element_type=jnp.float32,
        )
        summed = summed + term.astype(jnp.bfloat16).astype(jnp.float32)
    return summed.astype(jnp.bfloat16)


def solution(mesh):
    return jax.shard_map(
        local,
        mesh=mesh,
        in_specs=(
            P("seq", "head"),
            P("seq", "head"),
            P("seq", "head"),
            P("seq", "head"),
            P("head", "seq"),
        ),
        out_specs=P("seq", "head"),
        check_vma=False,
    )
```

profile of v0, /device:TPU:0, one launch (start us, length us, event | category | flops | bytes accessed | tf_op | source)
XLA Modules:
  0.0 501.1 jit_solution(6816774058546927798)
XLA Ops:
  6.5 0.0 all-gather.5.cloned.1.call-start
  6.5 2.3 copy.21
  8.8 0.0 all-gather.5.cloned.1.call-update
  8.8 0.0 all-reduce.3.cloned.1.call-start
  8.9 6.5 %fusion.3 = f32[16,256,128]{2,1,0:T(8,128)} fusion(s32[1024,16]{0,1:T(8,128)} %param.8, bf16[1024,2048]{1,0:T(8,128)(2,1)} %param.5), kind=kOutput, calls=%fused_computation.8 | convolution fusion | flops 1077936128 | bytes 6356992 | tf_op jit(solution)/shard_map/thc,thd->hcd/dot_general | solution.py:21
  15.4 0.0 all-reduce.3.cloned.1.call-update
  15.4 123.3 %all-gather.5.cloned.1.call-done = bf16[2048,4096]{0,1:T(8,128)(2,1)} async-done(((bf16[2048,256]{0,1:T(8,128)(2,1)}), bf16[2048,4096]{0,1:T(8,128)(2,1)}) %all-gather.5.cloned.1.call-update) | async-done | bytes 16777232 | tf_op jit(solution)/shard_map/all_gather | solution.py:17
  138.7 0.0 copy-start.1
  138.7 9.8 %all-to-all-start = ((bf16[2048,2,2048]{0,2,1:T(8,128)(2,1)}), bf16[2048,2,2048]{0,2,1:T(8,128)(2,1)}, u32[]{:S(2)}, u32[]{:S(2)}) async-start(bf16[2048,2,2048]{0,2,1:T(8,128)(2,1)} %bitcast.41), calls=%async_computation | async-start | bytes 33554432 | tf_op jit(solution)/shard_map/all_to_all | solution.py:18
  148.5 0.0 all-reduce.5.cloned.1.call-start
  148.6 0.0 copy-done.1
  148.6 1.8 convert_reduce_fusion.1
  150.4 59.4 %psum.29 = f32[16,256]{1,0:T(8,128)S(1)} all-reduce(f32[16,256]{1,0:T(8,128)S(1)} %convert_reduce_fusion.1), channel_id=1, replica_groups=mesh['seq'=16,'head'=2] {'seq'}, use_global_device_ids=true, to_apply=%region_2.0 | all-reduce | flops 4096 | bytes 32768 | tf_op jit(solution)/shard_map/psum | solution.py:23
  209.8 29.0 %all-reduce.3.cloned.1.call-done = f32[16,256,128]{2,1,0:T(8,128)} async-done(((f32[16,256,128]{2,1,0:T(8,128)}), f32[16,256,128]{2,1,0:T(8,128)}) %all-reduce.3.cloned.1.call-update) | async-done | bytes 2097168 | tf_op jit(solution)/shard_map/psum | solution.py:23
  238.8 11.0 %multiply_reduce_fusion = (f32[16,256]{1,0:T(8,128)S(1)}, f32[16,256,1024]{2,1,0:T(8,128)}) fusion(f32[16,256,128]{2,1,0:T(8,128)} %all-reduce.3.cloned.1.call-done, f32[16,256]{1,0:T(8,128)S(1)} %psum.29, bf16[1024,2048]{1,0:T(8,128)(2,1)} %param.6), kind=kOutput, calls=%fused_computation.9 | convolution fusion | flops 1083174912 | bytes 23101440 | tf_op jit(solution)/shard_map/hcd,thd->hct/dot_general | solution.py:25
  249.8 58.6 %pmax.7 = f32[16,256]{1,0:T(8,128)S(1)} all-reduce(f32[16,256]{1,0:T(8,128)S(1)} %get-tuple-element.7), channel_id=1, replica_groups=mesh['seq'=16,'head'=2] {'seq'}, use_global_device_ids=true, to_apply=%region_4.0 | all-reduce | flops 4096 | bytes 32768 | tf_op jit(solution)/shard_map/pmax | solution.py:33
  308.4 0.0 copy-start
  308.4 7.8 %convert_reduce_fusion = f32[16,256]{1,0:T(8,128)S(1)} fusion(f32[16,256]{1,0:T(8,128)S(1)} %get-tuple-element.7, f32[16,256,1024]{2,1,0:T(8,128)} %get-tuple-element.8), kind=kLoop, calls=%fused_computation.3 | loop fusion | flops 20967424 | bytes 16809984 | tf_op jit(solution)/shard_map/reduce_sum | solution.py:29
  316.3 2.7 copy-done
  319.1 6.9 %fusion.20 = f32[16,256,128]{2,1,0:T(8,128)} fusion(f32[16,256,1024]{2,1,0:T(8,128)S(1)} %copy-done, f32[16,256]{1,0:T(8,128)S(1)} %get-tuple-element.7, f32[16,256]{1,0:T(8,128)S(1)} %get-tuple-element.6, bf16[1024,2048]{1,0:T(8,128)(2,1)} %param.7), kind=kOutput, calls=%fused_computation.29 | convolution fusion | flops 1086849024 | bytes 23101440 | tf_op jit(solution)/shard_map/hct,thd->hcd/dot_general | solution.py:30
  326.0 0.0 all-reduce.5.cloned.1.call-update
  326.0 0.0 all-gather.3.cloned.1.call-start
  326.0 58.3 %psum.31 = f32[16,256]{1,0:T(8,128)S(1)} all-reduce(f32[16,256]{1,0:T(8,128)S(1)} %get-tuple-element.5), channel_id=1, replica_groups=mesh['seq'=16,'head'=2] {'seq'}, use_global_device_ids=true, to_apply=%region_7.0 | all-reduce | flops 4096 | bytes 32768 | tf_op jit(solution)/shard_map/psum | solution.py:35
  384.4 37.5 %all-reduce.5.cloned.1.call-done = f32[16,256,128]{2,1,0:T(8,128)} async-done(((f32[16,256,128]{2,1,0:T(8,128)}), f32[16,256,128]{2,1,0:T(8,128)}) %all-reduce.5.cloned.1.call-update) | async-done | bytes 2097168 | tf_op jit(solution)/shard_map/psum | solution.py:35
  421.8 2.7 divide_convert_fusion
  424.6 0.0 all-gather.3.cloned.1.call-update
  424.6 4.9 all_gather.10
  429.5 27.6 %all-gather.3.cloned.1.call-done = bf16[32,256,128]{2,1,0:T(8,128)(2,1)} async-done(((bf16[16,256,128]{2,1,0:T(8,128)(2,1)}), bf16[32,256,128]{2,1,0:T(8,128)(2,1)}) %all-gather.3.cloned.1.call-update) | async-done | bytes 2097168 | tf_op jit(solution)/shard_map/all_gather | solution.py:37
  457.1 12.0 %fusion.7 = bf16[32,128,1024]{2,1,0:T(8,128)(2,1)} fusion(bf16[32,256,128]{2,1,0:T(8,128)(2,1)} %all-gather.3.cloned.1.call-done, s32[1024,32]{0,1:T(8,128)S(1)} %all_gather.10), kind=kOutput, calls=%fused_computation.16 | convolution fusion | flops 2160066560 | bytes 10616832 | tf_op jit(solution)/shard_map/thc,hcd->thd/dot_general | solution.py:39
  469.1 0.0 all-to-all-done
  469.2 0.0 copy-start.2
  469.2 12.7 %fusion.4 = bf16[1024,2048]{1,0:T(8,128)(2,1)S(1)} fusion(bf16[2,2048,2048]{1,2,0:T(8,128)(2,1)} %bitcast.3, bf16[1024,4096]{0,1:T(8,128)(2,1)} %bitcast.42), kind=kOutput, calls=%fused_computation.11 | convolution fusion | flops 8589934592 | bytes 16777216 | tf_op jit(solution)/shard_map/dot_general | solution.py:47
  481.9 0.0 copy-done.2
  481.9 12.7 %add_convert_fusion = bf16[1024,2048]{1,0:T(8,128)(2,1)} fusion(bf16[1024,2048]{1,0:T(8,128)(2,1)S(1)} %fusion.4, bf16[2,2048,2048]{1,2,0:T(8,128)(2,1)} %bitcast.3, bf16[1024,4096]{0,1:T(8,128)(2,1)S(1)} %bitcast.43), kind=kOutput, calls=%fused_computation.14 | convolution fusion | flops 8600420352 | bytes 20971520 | tf_op jit(solution)/shard_map/dot_general | solution.py:47
  (1 shorter events, 0.0 us)
Async XLA Ops:
  6.5 132.1 %all-gather.5.cloned.1.call-start = ((), (), s32[]{:S(2)}) async-start(), calls=%async_computation.4 | async-start | bytes 17825792 | tf_op jit(solution)/shard_map/all_gather | solution.py:17
  8.8 230.0 %all-reduce.3.cloned.1.call-start = ((), (), s32[]{:S(2)}) async-start(), calls=%async_computation.1 | async-start | bytes 4194304 | tf_op jit(solution)/shard_map/psum | solution.py:23
  138.7 9.9 %copy-start.1 = (s32[1024,16]{0,1:T(8,128)S(1)}, s32[1024,16]{0,1:T(8,128)}, u32[]{:S(2)}) copy-start(s32[1024,16]{0,1:T(8,128)} %param.8) | copy-start | bytes 196612
  138.7 330.5 %all-to-all-start = ((bf16[2048,2,2048]{0,2,1:T(8,128)(2,1)}), bf16[2048,2,2048]{0,2,1:T(8,128)(2,1)}, u32[]{:S(2)}, u32[]{:S(2)}) async-start(bf16[2048,2,2048]{0,2,1:T(8,128)(2,1)} %bitcast.41), calls=%async_computation | async-start | bytes 33554432 | tf_op jit(solution)/shard_map/all_to_all | solution.py:18
  148.5 273.3 %all-reduce.5.cloned.1.call-start = ((), (), s32[]{:S(2)}) async-start(), calls=%async_computation.2 | async-start | bytes 4194304 | tf_op jit(solution)/shard_map/psum | solution.py:35
  308.4 10.6 %copy-start = (f32[16,256,1024]{2,1,0:T(8,128)S(1)}, f32[16,256,1024]{2,1,0:T(8,128)}, u32[]{:S(2)}) copy-start(f32[16,256,1024]{2,1,0:T(8,128)} %get-tuple-element.8) | copy-start | bytes 50331652
  326.0 131.1 %all-gather.3.cloned.1.call-start = ((), (), s32[]{:S(2)}) async-start(), calls=%async_computation.3 | async-start | bytes 3145728 | tf_op jit(solution)/shard_map/all_gather | solution.py:37
  469.2 12.7 %copy-start.2 = (bf16[32,128,1024]{2,1,0:T(8,128)(2,1)S(1)}, bf16[32,128,1024]{2,1,0:T(8,128)(2,1)}, u32[]{:S(2)}) copy-start(bf16[32,128,1024]{2,1,0:T(8,128)(2,1)} %fusion.7) | copy-start | bytes 25165828
Sparse Core Ops, SparseCore 0:
  9.5 129.1 all-gather.4
  142.2 96.5 all-reduce.2
  326.1 95.6 all-reduce.4
  424.7 32.3 all-gather.2
where the time goes:
time: 501 us
  waiting for transfers between devices  217 us (43%)
  blocking collectives  181 us (36%)
  matrix products  61.9 us (12%)
  between operations  13.2 us (3%)
  other arithmetic  12.4 us (2%)
  starting transfers between devices  9.94 us (2%)
  local copies, waits for them, and re-layouts  5.03 us (1%)
    all_gather x1, waiting for transfers between devices, local(): wide_rows = lax.all_gather(out_weight, 'seq', axis=1, tiled=True)  123 us
    psum x1, blocking collectives, local(): all_totals, all_counts = lax.psum((totals, counts), 'seq')  59.4 us
    pmax x1, blocking collectives, local(): global_peak = lax.pmax(block_peak, 'seq')  58.6 us
    psum x1, blocking collectives, local(): lax.psum((block_mass * factor, block_output * factor[:, :, None]), 'seq')  58.3 us
    psum x1, waiting for transfers between devices, local(): lax.psum((block_mass * factor, block_output * factor[:, :, None]), 'seq')  37.5 us
    psum x1, waiting for transfers between devices, local(): all_totals, all_counts = lax.psum((totals, counts), 'seq')  29 us
    all_gather x1, waiting for transfers between devices, local(): centre_every = lax.all_gather(centroid_out, 'head', axis=0, tiled=True)  27.6 us
    dot_general x2, matrix products, local(): jnp.dot(attended_all[:, group * group_rows:(group + 1) * group_rows], col...  25.4 us
  transfers between devices with their start and end apart: 5, of which 4 were waited for; matrix products, arithmetic and copies ran while one was open for 10% of the time, Pallas kernels for 0%

commit v1 on v0

v1 whole, which is shorter than its diff:
```python
import functools

import jax
import jax.numpy as jnp
from jax import lax
from jax.experimental import pallas as pl
from jax.experimental.pallas import tpu as pltpu
from jax.sharding import PartitionSpec as P

HDIM = 128
CLUSTERS = 256
LANES = 128
STAT = 8
MESH = pl.DeviceIdType.MESH


def columns_of(row):
    return jnp.broadcast_to(row, (LANES, LANES)).T


def greet(seq, bits, heads_n, with_heads):
    barrier = pltpu.get_barrier_semaphore()
    for bit in range(bits):
        partner = seq + (1 << bit) * (1 - 2 * (lax.rem(seq // (1 << bit), 2)))
        pl.semaphore_signal(barrier, inc=1, device_id={"seq": partner}, device_id_type=MESH)
    others = 0
    if with_heads:
        head = lax.axis_index("head")
        for step in range(1, heads_n):
            pl.semaphore_signal(
                barrier, inc=1, device_id={"head": lax.rem(head + step, heads_n)}, device_id_type=MESH
            )
            others += 1
    pl.semaphore_wait(barrier, bits + others)


def flip(seq, bit):
    digit = lax.rem(seq // (1 << bit), 2)
    return digit, seq + (1 << bit) * (1 - 2 * digit)


def halve(seq, bits, total, acc, recvs, send_sem, recv_sem, merge):
    start = jnp.int32(0)
    starts = [start]
    for bit in range(bits):
        half = total >> (bit + 1)
        digit, partner = flip(seq, bit)
        keep = start + digit * half
        give = start + (1 - digit) * half
        copy = pltpu.make_async_remote_copy(
            src_ref=acc.at[pl.ds(give, half)],
            dst_ref=recvs[bit],
            send_sem=send_sem.at[bit],
            recv_sem=recv_sem.at[bit],
            device_id={"seq": partner},
            device_id_type=MESH,
        )
        copy.start()
        copy.wait()

        def body(i, carry, keep=keep, bit=bit):
            merge(keep + i, recvs[bit], i)
            return carry

        lax.fori_loop(0, half, body, 0)
        start = keep
        starts.append(start)
    return starts


def double(seq, bits, total, starts, views, send_sem, recv_sem):
    for bit in range(bits - 1, -1, -1):
        size = total >> (bit + 1)
        _, partner = flip(seq, bit)
        copies = []
        for number, view in enumerate(views):
            part = view.at[pl.ds(starts[bit + 1], size)]
            copies.append(
                pltpu.make_async_remote_copy(
                    src_ref=part,
                    dst_ref=part,
                    send_sem=send_sem.at[bit, number],
                    recv_sem=recv_sem.at[bit, number],
                    device_id={"seq": partner},
                    device_id_type=MESH,
                )
            )
        for copy in copies:
            copy.start()
        for copy in copies:
            copy.wait()


def centre_kernel(n, bits, heads_n, rows, part_ref, ids_ref, out_ref, ids_out_ref, *scratch):
    acc, ids_all, full = scratch[:3]
    recvs = scratch[3 : 3 + bits]
    send_sem, recv_sem, gsend, grecv, isend, irecv, local_sem = scratch[3 + bits :]
    seq = lax.axis_index("seq")
    head = lax.axis_index("head")
    load = pltpu.make_async_copy(part_ref, acc, local_sem.at[0])
    load.start()
    own = pltpu.make_async_copy(ids_ref, ids_all.at[head], local_sem.at[1])
    own.start()
    greet(seq, bits, heads_n, True)
    id_copies = []
    for step in range(1, heads_n):
        copy = pltpu.make_async_remote_copy(
            src_ref=ids_ref,
            dst_ref=ids_all.at[head],
            send_sem=isend.at[step - 1],
            recv_sem=irecv.at[step - 1],
            device_id={"head": lax.rem(head + step, heads_n)},
            device_id_type=MESH,
        )
        copy.start()
        id_copies.append(copy)
    load.wait()

    def merge(chunk, recv, i):
        acc[chunk] = acc[chunk] + recv[i]

    starts = halve(seq, bits, n, acc, recvs, send_sem, recv_sem, merge)
    mine = starts[-1]
    block = min(rows, LANES)
    for b in range(rows // block):
        count = columns_of(acc[mine, rows + b : rows + b + 1, :])[:block]
        full[mine, b * block : (b + 1) * block, :] = (
            acc[mine, b * block : (b + 1) * block, :] / count
        ).astype(jnp.bfloat16)
    double(seq, bits, n, starts, [full], gsend, grecv)
    out_ref[...] = full[...]
    own.wait()
    for copy in id_copies:
        copy.wait()
    ids_out_ref[...] = ids_all[...]


def output_kernel(n, bits, heads_n, rows, part_ref, out_ref, *scratch):
    acc, full = scratch[:2]
    recvs = scratch[2 : 2 + bits]
    send_sem, recv_sem, gsend, grecv, hsend, hrecv, local_sem = scratch[2 + bits :]
    seq = lax.axis_index("seq")
    head = lax.axis_index("head")
    load = pltpu.make_async_copy(part_ref, acc, local_sem.at[0])
    load.start()
    greet(seq, bits, heads_n, True)
    load.wait()
    block = min(rows, LANES)

    def merge(chunk, recv, i):
        mine = acc[chunk, rows : rows + STAT, :]
        other = recv[i, rows : rows + STAT, :]
        for b in range(rows // block):
            peak_a, peak_b = mine[b : b + 1], other[b : b + 1]
            peak = jnp.maximum(peak_a, peak_b)
            scale_a, scale_b = jnp.exp(peak_a - peak), jnp.exp(peak_b - peak)
            acc[chunk, rows + b : rows + b + 1, :] = peak
            acc[chunk, rows + 4 + b : rows + 5 + b, :] = (
                scale_a * mine[4 + b : 5 + b] + scale_b * other[4 + b : 5 + b]
            )
            span = slice(b * block, (b + 1) * block)
            acc[chunk, span, :] = (
                acc[chunk, span, :] * columns_of(scale_a)[:block]
                + recv[i, span, :] * columns_of(scale_b)[:block]
            )

    starts = halve(seq, bits, n, acc, recvs, send_sem, recv_sem, merge)
    mine = starts[-1]
    for b in range(rows // block):
        mass = columns_of(acc[mine, rows + 4 + b : rows + 5 + b, :])[:block]
        full[head, mine, b * block : (b + 1) * block, :] = (
            acc[mine, b * block : (b + 1) * block, :] / mass
        ).astype(jnp.bfloat16)
    copies = []
    for step in range(1, heads_n):
        part = full.at[head, mine]
        copies.append(
            pltpu.make_async_remote_copy(
                src_ref=part,
                dst_ref=part,
                send_sem=hsend.at[step - 1],
                recv_sem=hrecv.at[step - 1],
                device_id={"head": lax.rem(head + step, heads_n)},
                device_id_type=MESH,
            )
        )
    for copy in copies:
        copy.start()
    for copy in copies:
        copy.wait()
    double(seq, bits, n, starts, [full.at[h] for h in range(heads_n)], gsend, grecv)
    out_ref[...] = full[...]


def local(queries, keys, values, cluster_ids, out_weight):
    n = lax.axis_size("seq")
    heads_n = lax.axis_size("head")
    bits = n.bit_length() - 1
    token_rows = queries.shape[0]
    head_count = queries.shape[1] // HDIM
    rows = head_count * CLUSTERS // n
    blocks = max(rows // LANES, 1)
    query_three = queries.reshape(token_rows, head_count, HDIM)
    key_three = keys.reshape(token_rows, head_count, HDIM)
    value_three = values.reshape(token_rows, head_count, HDIM)
    labels = jnp.arange(CLUSTERS, dtype=jnp.int32)

    low = n // heads_n
    wide = lax.all_gather(
        out_weight, "seq", axis=0, axis_index_groups=[[g * low + r for g in range(heads_n)] for r in range(low)]
    )
    tall = lax.all_to_all(wide, "head", split_axis=0, concat_axis=0, tiled=True)
    tall = tall.reshape(-1, out_weight.shape[1])
    column_weight = lax.all_gather(
        tall, "seq", axis=1, tiled=True,
        axis_index_groups=[[g * low + r for r in range(low)] for g in range(heads_n)],
    )

    ids_t = cluster_ids.T
    member = (ids_t[:, None, :] == labels[None, :, None]).astype(jnp.bfloat16)
    totals = jnp.einsum("hct,thd->hcd", member, query_three, preferred_element_type=jnp.float32)
    counts = jnp.sum(member, axis=2, dtype=jnp.float32)

    def lanes(stat):
        stat = stat.reshape(n, blocks, rows // blocks)
        return jnp.pad(stat, ((0, 0), (0, 0), (0, LANES - rows // blocks)))

    def stats(arrays):
        each = STAT // len(arrays)
        return jnp.concatenate(
            [jnp.pad(lanes(a), ((0, 0), (0, each - blocks), (0, 0))) for a in arrays], axis=1
        )

    def packed(big, arrays):
        return jnp.concatenate([big.reshape(n, rows, HDIM), stats(arrays)], axis=1)

    vmem = pl.BlockSpec(memory_space=pltpu.VMEM)
    anywhere = pl.BlockSpec(memory_space=pl.ANY)
    dma = pltpu.SemaphoreType.DMA
    recvs = [pltpu.VMEM((n >> (bit + 1), rows + STAT, LANES), jnp.float32) for bit in range(bits)]
    others = max(heads_n - 1, 1)
    centre, ids_every = pl.pallas_call(
        functools.partial(centre_kernel, n, bits, heads_n, rows),
        out_shape=(
            jax.ShapeDtypeStruct((n, rows, HDIM), jnp.bfloat16),
            jax.ShapeDtypeStruct((heads_n, head_count, token_rows), jnp.int32),
        ),
        in_specs=[anywhere, vmem],
        out_specs=(vmem, vmem),
        scratch_shapes=[
            pltpu.VMEM((n, rows + STAT, LANES), jnp.float32),
            pltpu.VMEM((heads_n, head_count, token_rows), jnp.int32),
            pltpu.VMEM((n, rows, HDIM), jnp.bfloat16),
            *recvs,
            dma((bits,)), dma((bits,)), dma((bits, 1)), dma((bits, 1)),
            dma((others,)), dma((others,)), dma((2,)),
        ],
        compiler_params=pltpu.CompilerParams(collective_id=0, has_side_effects=True),
    )(packed(totals, [counts]), ids_t)
    centre = centre.reshape(head_count, CLUSTERS, HDIM)

    scores = jnp.einsum("hcd,thd->hct", centre, key_three, preferred_element_type=jnp.float32)
    scores = scores * (1.0 / HDIM**0.5)
    block_peak = jnp.max(scores, axis=2)
    weights = jnp.exp(scores - block_peak[:, :, None]).astype(jnp.bfloat16)
    block_mass = jnp.sum(weights, axis=2, dtype=jnp.float32)
    block_output = jnp.einsum(
        "hct,thd->hcd", weights, value_three, preferred_element_type=jnp.float32
    )

    centre_every = pl.pallas_call(
        functools.partial(output_kernel, n, bits, heads_n, rows),
        out_shape=jax.ShapeDtypeStruct((heads_n, n, rows, HDIM), jnp.bfloat16),
        in_specs=[anywhere],
        out_specs=vmem,
        scratch_shapes=[
            pltpu.VMEM((n, rows + STAT, LANES), jnp.float32),
            pltpu.VMEM((heads_n, n, rows, HDIM), jnp.bfloat16),
            *recvs,
            dma((bits,)), dma((bits,)), dma((bits, heads_n)), dma((bits, heads_n)),
            dma((others,)), dma((others,)), dma((1,)),
        ],
        compiler_params=pltpu.CompilerParams(collective_id=1, has_side_effects=True),
    )(packed(block_output, [block_peak, block_mass]))
    centre_every = centre_every.reshape(heads_n * head_count, CLUSTERS, HDIM)

    ids_every = ids_every.reshape(heads_n * head_count, token_rows)
    member_every = (ids_every[:, None, :] == labels[None, :, None]).astype(jnp.bfloat16)
    attended_all = jnp.einsum(
        "hct,hcd->thd", member_every, centre_every, preferred_element_type=jnp.float32
    )
    attended_all = attended_all.astype(jnp.bfloat16).reshape(token_rows, -1)
    group_rows = attended_all.shape[1] // heads_n
    summed = jnp.zeros((token_rows, column_weight.shape[1]), jnp.float32)
    for group in range(heads_n):
        term = jnp.dot(
            attended_all[:, group * group_rows : (group + 1) * group_rows],
            column_weight[group * group_rows : (group + 1) * group_rows, :],
            preferred_element_type=jnp.float32,
        )
        summed = summed + term.astype(jnp.bfloat16).astype(jnp.float32)
    return summed.astype(jnp.bfloat16)


def solution(mesh):
    return jax.shard_map(
        local,
        mesh=mesh,
        in_specs=(
            P("seq", "head"),
            P("seq", "head"),
            P("seq", "head"),
            P("seq", "head"),
            P("head", "seq"),
        ),
        out_specs=P("seq", "head"),
        check_vma=False,
    )
```

time: 501 us -> 315 us (0.63)
  waiting for transfers between devices: 217 us -> 61.6 us
  blocking collectives: 181 us -> 30.6 us
  Pallas kernels: 0 us -> 133 us
  starting transfers between devices: 9.94 us -> 0.04 us
    pallas_call x0 -> x2, Pallas kernels: none -> 133 us  [the longest x1 68.6 us: local(): pl.pallas_call(functools.partial(centre_kernel, n, bits, heads_n, rows),...]
    psum x2 -> x0, blocking collectives: 118 us -> none  [the longest x1 59.4 us: local(): all_totals, all_counts = lax.psum((totals, counts), 'seq')]
    all_gather x2, waiting for transfers between devices: 151 us -> 60.8 us  [the longest x1 60.8 us: local(): lax.all_gather(out_weight, 'seq', axis=0, axis_index_groups=[[g * low + r...]
    psum x2 -> x0, waiting for transfers between devices: 66.5 us -> none  [the longest x1 37.5 us: local(): lax.psum((block_mass * factor, block_output * factor[:, :, None]), 'seq')]
    pmax x1 -> x0, blocking collectives: 58.6 us -> none  [local(): global_peak = lax.pmax(block_peak, 'seq')]
    all_to_all x0 -> x1, blocking collectives: none -> 30.6 us  [local(): tall = lax.all_to_all(wide, 'head', split_axis=0, concat_axis=0, tiled=True)]
    all_to_all x1 -> x0, starting transfers between devices: 9.81 us -> none  [local(): lax.all_to_all(wide_rows, 'head', split_axis=1, concat_axis=0, tiled=True)]
    unnamed x7 -> x6, local copies, waits for them, and re-layouts: 5.03 us -> 0.01 us
  transfers between devices with their start and end apart: 5 -> 2, of which waited for: 4 -> 1; matrix products, arithmetic and copies ran while one was open for 10% -> 16% of each run, Pallas kernels for 0% -> 42%
where the time goes in v1:
time: 315 us; the launch traced here: 314 us
  Pallas kernels  133 us (42%)
  matrix products  62.3 us (20%)
  waiting for transfers between devices  61.6 us (20%)
  blocking collectives  30.6 us (10%)
  between operations  13.5 us (4%)
  other arithmetic  12.6 us (4%)
    pallas_call x1, Pallas kernels, local(): pl.pallas_call(functools.partial(centre_kernel, n, bits, heads_n, rows),...  68.6 us
    pallas_call x1, Pallas kernels, local(): pl.pallas_call(functools.partial(output_kernel, n, bits, heads_n, rows),...  64.8 us
    all_gather x1, waiting for transfers between devices, local(): lax.all_gather(out_weight, 'seq', axis=0, axis_index_groups=[[g * low + r...  60.8 us
    all_to_all x1, blocking collectives, local(): tall = lax.all_to_all(wide, 'head', split_axis=0, concat_axis=0, tiled=True)  30.6 us
    dot_general x2, matrix products, local(): jnp.dot(attended_all[:, group * group_rows:(group + 1) * group_rows], col...  25.7 us
    dot_general x1, matrix products, local(): jnp.einsum('hcd,thd->hct', centre, key_three, preferred_element_type=jnp....  10.9 us
    dot_general x1, matrix products, local(): jnp.einsum('hct,hcd->thd', member_every, centre_every, preferred_element_...  10.8 us
    dot_general x1, matrix products, local(): jnp.einsum('hct,thd->hcd', weights, value_three, preferred_element_type=j...  9.75 us
  transfers between devices with their start and end apart: 2, of which 1 were waited for; matrix products, arithmetic and copies ran while one was open for 16% of the time, Pallas kernels for 42%

profile of v1, /device:TPU:0, one launch (start us, length us, event | category | flops | bytes accessed | tf_op | source)
XLA Modules:
  0.0 314.0 jit_solution(11353700408861270050)
XLA Ops:
  6.5 0.0 copy-start
  6.5 0.0 all-gather.6.cloned.1.call-start
  6.5 0.7 all-gather.6.cloned.1.call-update
  7.3 0.0 all-gather.4.cloned.1.call-start
  7.3 60.8 %all-gather.6.cloned.1.call-done = bf16[4096,256]{1,0:T(8,128)(2,1)} async-done(((bf16[2048,256]{1,0:T(8,128)(2,1)}), bf16[4096,256]{1,0:T(8,128)(2,1)}) %all-gather.6.cloned.1.call-update) | async-done | bytes 2097168 | tf_op jit(solution)/shard_map/all_gather | solution.py:209
  68.1 30.6 %all_to_all.5 = bf16[2,2048,256]{2,1,0:T(8,128)(2,1)} all-to-all(bf16[2,2048,256]{2,1,0:T(8,128)(2,1)} %bitcast.34), channel_id=1, replica_groups=mesh['seq'=16,'head'=2] {'head'}, dimensions={0} | all-to-all | bytes 4194304 | tf_op jit(solution)/shard_map/all_to_all | solution.py:212
  98.7 0.0 all-gather.4.cloned.1.call-update
  98.8 0.0 copy-done
  98.8 1.8 convert_reduce_fusion.1
  100.6 5.1 %fusion.3 = f32[16,256,128]{2,1,0:T(8,128)S(1)} fusion(s32[16,1024]{1,0:T(8,128)S(1)} %bitcast.38, bf16[1024,2048]{1,0:T(8,128)(2,1)} %param.5), kind=kOutput, calls=%fused_computation.8 | convolution fusion | flops 1077936128 | bytes 6356992 | tf_op jit(solution)/shard_map/hct,thd->hcd/dot_general | solution.py:221
  105.8 1.5 select_maximum_fusion.2.part_ref
  107.3 68.6 %shard_map.55 = (bf16[16,256,128]{2,1,0:T(8,128)(2,1)}, s32[2,16,1024]{2,1,0:T(8,128)}) custom-call(f32[16,264,128]{2,1,0:T(8,128)} %select_maximum_fusion.2.part_ref, s32[16,1024]{1,0:T(8,128)} %bitcast.36), custom_call_target="tpu_custom_call" | custom-call | tf_op jit(solution)/shard_map/pallas_call | solution.py:242
  175.9 10.9 %multiply_reduce_fusion = (f32[16,256]{1,0:T(8,128)S(1)}, f32[16,256,1024]{2,1,0:T(8,128)}) fusion(bf16[16,256,128]{2,1,0:T(8,128)(2,1)} %get-tuple-element.7, bf16[1024,2048]{1,0:T(8,128)(2,1)} %param.6), kind=kOutput, calls=%fused_computation.9 | convolution fusion | flops 1082126336 | bytes 22036480 | tf_op jit(solution)/shard_map/hcd,thd->hct/dot_general | solution.py:262
  186.8 7.8 %convert_reduce_fusion = f32[16,256]{1,0:T(8,128)S(1)} fusion(f32[16,256]{1,0:T(8,128)S(1)} %get-tuple-element.9, f32[16,256,1024]{2,1,0:T(8,128)} %get-tuple-element.10), kind=kLoop, calls=%fused_computation.3 | loop fusion | flops 20967424 | bytes 16809984 | tf_op jit(solution)/shard_map/reduce_sum | solution.py:266
  194.6 9.8 %fusion.10 = f32[16,256,128]{2,1,0:T(8,128)S(1)} fusion(f32[16,256,1024]{2,1,0:T(8,128)} %get-tuple-element.10, f32[16,256]{1,0:T(8,128)S(1)} %get-tuple-element.9, bf16[1024,2048]{1,0:T(8,128)(2,1)} %param.7), kind=kOutput, calls=%fused_computation.17 | convolution fusion | flops 1086324736 | bytes 23085056 | tf_op jit(solution)/shard_map/hct,thd->hcd/dot_general | solution.py:267
  204.3 0.0 copy-start.2
  204.4 1.5 select_maximum_fusion.part_ref
  205.8 64.8 %shard_map.56 = bf16[2,16,256,128]{3,2,1,0:T(8,128)(2,1)} custom-call(f32[16,264,128]{2,1,0:T(8,128)} %select_maximum_fusion.part_ref), custom_call_target="tpu_custom_call" | custom-call | tf_op jit(solution)/shard_map/pallas_call | solution.py:271
  270.6 0.0 copy-done.2
  270.6 10.8 %fusion.9 = bf16[32,128,1024]{2,1,0:T(8,128)(2,1)} fusion(bf16[32,256,128]{2,1,0:T(8,128)(2,1)} %bitcast.35, s32[32,1024]{1,0:T(8,128)S(1)} %bitcast.39), kind=kOutput, calls=%fused_computation.16 | convolution fusion | flops 2160066560 | bytes 10616832 | tf_op jit(solution)/shard_map/hct,hcd->thd/dot_general | solution.py:289
  281.5 0.0 all-gather.4.cloned.1.call-done
  281.5 0.0 copy-start.1
  281.5 12.8 %fusion.4 = bf16[1024,2048]{1,0:T(8,128)(2,1)S(1)} fusion(bf16[4096,2048]{1,0:T(8,128)(2,1)} %all-gather.4.cloned.1.call-done, bf16[1024,4096]{0,1:T(8,128)(2,1)} %bitcast.40), kind=kOutput, calls=%fused_computation.10 | convolution fusion | flops 8589934592 | bytes 16777216 | tf_op jit(solution)/shard_map/dot_general | solution.py:296
  294.3 0.0 copy-done.1
  294.3 12.9 %add_convert_fusion = bf16[1024,2048]{1,0:T(8,128)(2,1)} fusion(bf16[1024,2048]{1,0:T(8,128)(2,1)S(1)} %fusion.4, bf16[4096,2048]{1,0:T(8,128)(2,1)S(1)} %copy-done.1, bf16[1024,4096]{0,1:T(8,128)(2,1)} %bitcast.41), kind=kOutput, calls=%fused_computation.14 | convolution fusion | flops 8600420352 | bytes 20971520 | tf_op jit(solution)/shard_map/dot_general | solution.py:296
  (3 shorter events, 0.0 us)
Async XLA Ops:
  6.5 92.2 %copy-start = (s32[1024,16]{0,1:T(8,128)S(1)}, s32[1024,16]{0,1:T(8,128)}, u32[]{:S(2)}) copy-start(s32[1024,16]{0,1:T(8,128)} %param.8) | copy-start | bytes 196612
  6.5 61.6 %all-gather.6.cloned.1.call-start = ((), (), s32[]{:S(2)}) async-start(), calls=%async_computation.2 | async-start | bytes 3145728 | tf_op jit(solution)/shard_map/all_gather | solution.py:209
  7.3 274.2 %all-gather.4.cloned.1.call-start = ((), (), s32[]{:S(2)}) async-start(), calls=%async_computation.1 | async-start | bytes 18874368 | tf_op jit(solution)/shard_map/all_gather | solution.py:214
  204.3 66.3 %copy-start.2 = (s32[2,16,1024]{2,1,0:T(8,128)S(1)}, s32[2,16,1024]{2,1,0:T(8,128)}, u32[]{:S(2)}) copy-start(s32[2,16,1024]{2,1,0:T(8,128)} %get-tuple-element.8) | copy-start | bytes 393220
  281.5 12.8 %copy-start.1 = (bf16[4096,2048]{1,0:T(8,128)(2,1)S(1)}, bf16[4096,2048]{1,0:T(8,128)(2,1)}, u32[]{:S(2)}) copy-start(bf16[4096,2048]{1,0:T(8,128)(2,1)} %all-gather.4.cloned.1.call-done) | copy-start | bytes 50331652
Sparse Core Ops, SparseCore 0:
  8.9 59.2 all-gather.5
  98.9 104.3 all-gather.3

commit v2 on v1

v2 whole, which is shorter than its diff:
```python
import functools

import jax
import jax.numpy as jnp
from jax import lax
from jax.experimental import pallas as pl
from jax.experimental.pallas import tpu as pltpu
from jax.sharding import PartitionSpec as P

HDIM = 128
CLUSTERS = 256
LANES = 128
STAT = 8
MESH = pl.DeviceIdType.MESH


def columns_of(row):
    return jnp.broadcast_to(row, (LANES, LANES)).T


def flip(seq, bit):
    digit = lax.rem(seq // (1 << bit), 2)
    return digit, seq + (1 << bit) * (1 - 2 * digit)


def orders_of(bits):
    straight = list(range(bits))
    return [straight, straight[:1] + straight[2:] + straight[1:2]]


def greet(seq, bits, heads_n, digits):
    barrier = pltpu.get_barrier_semaphore()
    head = lax.axis_index("head")
    n = 1 << bits
    targets = [{"seq": flip(seq, bit)[1]} for bit in range(bits)]
    targets += [{"head": lax.rem(head + step, heads_n)} for step in range(1, heads_n)]
    if digits:
        low = n // heads_n
        targets += [{"seq": lax.rem(seq + step * low, n)} for step in range(1, heads_n)]
    for target in targets:
        pl.semaphore_signal(barrier, inc=1, device_id=target, device_id_type=MESH)
    pl.semaphore_wait(barrier, len(targets))


def halve(seq, bits, acc, recvs, send_sem, recv_sem, merge):
    n = 1 << bits
    orders = orders_of(bits)
    starts = [[jnp.int32(0)] for _ in orders]

    def begin(stream, step):
        half = n >> (step + 1)
        digit, partner = flip(seq, orders[stream][step])
        start = starts[stream][step]
        give = start + (1 - digit) * half
        starts[stream].append(start + digit * half)
        copy = pltpu.make_async_remote_copy(
            src_ref=acc.at[stream, pl.ds(give, half)],
            dst_ref=recvs[step].at[stream],
            send_sem=send_sem.at[stream, step],
            recv_sem=recv_sem.at[stream, step],
            device_id={"seq": partner},
            device_id_type=MESH,
        )
        copy.start()
        return copy

    pending = [begin(stream, 0) for stream in range(len(orders))]
    for step in range(bits):
        for stream in range(len(orders)):
            pending[stream].wait()
            keep = starts[stream][step + 1]

            def body(i, carry, stream=stream, keep=keep, step=step):
                merge(stream, keep + i, recvs[step], i)
                return carry

            lax.fori_loop(0, n >> (step + 1), body, 0)
            if step + 1 < bits:
                pending[stream] = begin(stream, step + 1)
    return starts


def double(seq, bits, starts, views, send_sem, recv_sem):
    n = 1 << bits
    orders = orders_of(bits)

    def begin(stream, step):
        _, partner = flip(seq, orders[stream][step])
        copies = []
        for number, view in enumerate(views):
            part = view.at[stream, pl.ds(starts[stream][step + 1], n >> (step + 1))]
            copies.append(
                pltpu.make_async_remote_copy(
                    src_ref=part,
                    dst_ref=part,
                    send_sem=send_sem.at[stream, step, number],
                    recv_sem=recv_sem.at[stream, step, number],
                    device_id={"seq": partner},
                    device_id_type=MESH,
                )
            )
        for copy in copies:
            copy.start()
        return copies

    pending = [begin(stream, bits - 1) for stream in range(len(orders))]
    for step in range(bits - 1, -1, -1):
        for stream in range(len(orders)):
            for copy in pending[stream]:
                copy.wait()
            if step > 0:
                pending[stream] = begin(stream, step - 1)


def centre_kernel(
    bits, heads_n, rows, part_ref, ids_ref, weight_ref, out_ref, ids_out_ref, tall_ref, *scratch
):
    acc, ids_all, full, wide, tall = scratch[:5]
    recvs = scratch[5 : 5 + bits]
    send_sem, recv_sem, gsend, grecv, isend, irecv, zsend, zrecv, ysend, yrecv, local_sem, put_sem = scratch[
        5 + bits :
    ]
    seq = lax.axis_index("seq")
    head = lax.axis_index("head")
    n = 1 << bits
    low = n // heads_n
    group = seq // low
    load = pltpu.make_async_copy(part_ref, acc, local_sem.at[0])
    load.start()
    own = pltpu.make_async_copy(ids_ref, ids_all.at[head], local_sem.at[1])
    own.start()
    own_weight = pltpu.make_async_copy(weight_ref, wide.at[group], local_sem.at[2])
    own_weight.start()
    greet(seq, bits, heads_n, True)

    def to_head(step, src, dst, sends, receives):
        return pltpu.make_async_remote_copy(
            src_ref=src,
            dst_ref=dst,
            send_sem=sends.at[step - 1],
            recv_sem=receives.at[step - 1],
            device_id={"head": lax.rem(head + step, heads_n)},
            device_id_type=MESH,
        )

    load.wait()
    across = []
    for step in range(1, heads_n):
        across.append(
            pltpu.make_async_remote_copy(
                src_ref=weight_ref,
                dst_ref=wide.at[group],
                send_sem=zsend.at[step - 1],
                recv_sem=zrecv.at[step - 1],
                device_id={"seq": lax.rem(seq + step * low, n)},
                device_id_type=MESH,
            )
        )
    id_copies = [to_head(step, ids_ref, ids_all.at[head], isend, irecv) for step in range(1, heads_n)]
    for copy in across + id_copies:
        copy.start()

    def merge(stream, chunk, recv, i):
        acc[stream, chunk] = acc[stream, chunk] + recv[stream, i]

    starts = halve(seq, bits, acc, recvs, send_sem, recv_sem, merge)
    block = min(rows, LANES)
    for stream in range(2):
        mine = starts[stream][-1]
        for b in range(rows // block):
            span = slice(b * block, (b + 1) * block)
            count = columns_of(acc[stream, mine, rows + b : rows + b + 1, :])[:block]
            full[stream, mine, span, :] = (acc[stream, mine, span, :] / count).astype(jnp.bfloat16)
    own_weight.wait()
    for copy in across:
        copy.wait()
    beside = [to_head(s, wide.at[lax.rem(head + s, heads_n)], tall.at[head], ysend, yrecv) for s in range(1, heads_n)]
    for copy in beside:
        copy.start()
    puts = [pltpu.make_async_copy(wide.at[head], tall_ref.at[head], put_sem.at[0])]
    puts[0].start()
    double(seq, bits, starts, [full], gsend, grecv)
    out_ref[...] = full[...]
    own.wait()
    for copy in id_copies:
        copy.wait()
    ids_out_ref[...] = ids_all[...]
    for copy in beside:
        copy.wait()
    for step in range(1, heads_n):
        other = lax.rem(head + step, heads_n)
        puts.append(pltpu.make_async_copy(tall.at[other], tall_ref.at[other], put_sem.at[step]))
        puts[-1].start()
    for put in puts:
        put.wait()


def output_kernel(bits, heads_n, rows, part_ref, out_ref, *scratch):
    acc, full = scratch[:2]
    recvs = scratch[2 : 2 + bits]
    send_sem, recv_sem, gsend, grecv, hsend, hrecv, local_sem = scratch[2 + bits :]
    seq = lax.axis_index("seq")
    head = lax.axis_index("head")
    load = pltpu.make_async_copy(part_ref, acc, local_sem.at[0])
    load.start()
    greet(seq, bits, heads_n, False)
    load.wait()
    block = min(rows, LANES)

    def merge(stream, chunk, recv, i):
        mine = acc[stream, chunk, rows : rows + STAT, :]
        other = recv[stream, i, rows : rows + STAT, :]
        for b in range(rows // block):
            peak_a, peak_b = mine[b : b + 1], other[b : b + 1]
            peak = jnp.maximum(peak_a, peak_b)
            scale_a, scale_b = jnp.exp(peak_a - peak), jnp.exp(peak_b - peak)
            acc[stream, chunk, rows + b : rows + b + 1, :] = peak
            acc[stream, chunk, rows + 4 + b : rows + 5 + b, :] = (
                scale_a * mine[4 + b : 5 + b] + scale_b * other[4 + b : 5 + b]
            )
            span = slice(b * block, (b + 1) * block)
            acc[stream, chunk, span, :] = (
                acc[stream, chunk, span, :] * columns_of(scale_a)[:block]
                + recv[stream, i, span, :] * columns_of(scale_b)[:block]
            )

    starts = halve(seq, bits, acc, recvs, send_sem, recv_sem, merge)
    copies = []
    for stream in range(2):
        mine = starts[stream][-1]
        for b in range(rows // block):
            span = slice(b * block, (b + 1) * block)
            mass = columns_of(acc[stream, mine, rows + 4 + b : rows + 5 + b, :])[:block]
            full[head, stream, mine, span, :] = (acc[stream, mine, span, :] / mass).astype(jnp.bfloat16)
        part = full.at[head, stream, mine]
        for step in range(1, heads_n):
            copies.append(
                pltpu.make_async_remote_copy(
                    src_ref=part,
                    dst_ref=part,
                    send_sem=hsend.at[stream, step - 1],
                    recv_sem=hrecv.at[stream, step - 1],
                    device_id={"head": lax.rem(head + step, heads_n)},
                    device_id_type=MESH,
                )
            )
    for copy in copies:
        copy.start()
    for copy in copies:
        copy.wait()
    double(seq, bits, starts, [full.at[h] for h in range(heads_n)], gsend, grecv)
    out_ref[...] = full[...]


def local(queries, keys, values, cluster_ids, out_weight):
    n = lax.axis_size("seq")
    heads_n = lax.axis_size("head")
    bits = n.bit_length() - 1
    token_rows = queries.shape[0]
    head_count = queries.shape[1] // HDIM
    rows = head_count * CLUSTERS // n // 2
    blocks = max(rows // LANES, 1)
    query_three = queries.reshape(token_rows, head_count, HDIM)
    key_three = keys.reshape(token_rows, head_count, HDIM)
    value_three = values.reshape(token_rows, head_count, HDIM)
    labels = jnp.arange(CLUSTERS, dtype=jnp.int32)

    ids_t = cluster_ids.T
    member = (ids_t[:, None, :] == labels[None, :, None]).astype(jnp.bfloat16)
    totals = jnp.einsum("hct,thd->hcd", member, query_three, preferred_element_type=jnp.float32)
    counts = jnp.sum(member, axis=2, dtype=jnp.float32)

    def lanes(stat):
        stat = stat.reshape(2, n, blocks, rows // blocks)
        return jnp.pad(stat, ((0, 0), (0, 0), (0, 0), (0, LANES - rows // blocks)))

    def stats(arrays):
        each = STAT // len(arrays)
        return jnp.concatenate(
            [jnp.pad(lanes(a), ((0, 0), (0, 0), (0, each - blocks), (0, 0))) for a in arrays], axis=2
        )

    def packed(big, arrays):
        return jnp.concatenate([big.reshape(2, n, rows, HDIM), stats(arrays)], axis=2)

    vmem = pl.BlockSpec(memory_space=pltpu.VMEM)
    anywhere = pl.BlockSpec(memory_space=pl.ANY)
    dma = pltpu.SemaphoreType.DMA
    recvs = [pltpu.VMEM((2, n >> (bit + 1), rows + STAT, LANES), jnp.float32) for bit in range(bits)]
    others = max(heads_n - 1, 1)
    centre, ids_every, tall = pl.pallas_call(
        functools.partial(centre_kernel, bits, heads_n, rows),
        out_shape=(
            jax.ShapeDtypeStruct((2, n, rows, HDIM), jnp.bfloat16),
            jax.ShapeDtypeStruct((heads_n, head_count, token_rows), jnp.int32),
            jax.ShapeDtypeStruct((heads_n, *out_weight.shape), jnp.bfloat16),
        ),
        in_specs=[anywhere, vmem, anywhere],
        out_specs=(vmem, vmem, anywhere),
        scratch_shapes=[
            pltpu.VMEM((2, n, rows + STAT, LANES), jnp.float32),
            pltpu.VMEM((heads_n, head_count, token_rows), jnp.int32),
            pltpu.VMEM((2, n, rows, HDIM), jnp.bfloat16),
            pltpu.VMEM((heads_n, *out_weight.shape), jnp.bfloat16),
            pltpu.VMEM((heads_n, *out_weight.shape), jnp.bfloat16),
            *recvs,
            dma((2, bits)), dma((2, bits)), dma((2, bits, 1)), dma((2, bits, 1)),
            dma((others,)), dma((others,)), dma((others,)), dma((others,)), dma((others,)), dma((others,)),
            dma((3,)), dma((heads_n,)),
        ],
        compiler_params=pltpu.CompilerParams(collective_id=0, has_side_effects=True),
    )(packed(totals, [counts]), ids_t, out_weight)
    low = n // heads_n
    column_weight = lax.all_gather(
        tall.reshape(-1, out_weight.shape[1]), "seq", axis=1, tiled=True,
        axis_index_groups=[[g * low + r for r in range(low)] for g in range(heads_n)],
    )
    centre = centre.reshape(head_count, CLUSTERS, HDIM)

    scores = jnp.einsum("hcd,thd->hct", centre, key_three, preferred_element_type=jnp.float32)
    scores = scores * (1.0 / HDIM**0.5)
    block_peak = jnp.max(scores, axis=2)
    weights = jnp.exp(scores - block_peak[:, :, None]).astype(jnp.bfloat16)
    block_mass = jnp.sum(weights, axis=2, dtype=jnp.float32)
    block_output = jnp.einsum(
        "hct,thd->hcd", weights, value_three, preferred_element_type=jnp.float32
    )

    centre_every = pl.pallas_call(
        functools.partial(output_kernel, bits, heads_n, rows),
        out_shape=jax.ShapeDtypeStruct((heads_n, 2, n, rows, HDIM), jnp.bfloat16),
        in_specs=[anywhere],
        out_specs=vmem,
        scratch_shapes=[
            pltpu.VMEM((2, n, rows + STAT, LANES), jnp.float32),
            pltpu.VMEM((heads_n, 2, n, rows, HDIM), jnp.bfloat16),
            *recvs,
            dma((2, bits)), dma((2, bits)), dma((2, bits, heads_n)), dma((2, bits, heads_n)),
            dma((2, others)), dma((2, others)), dma((1,)),
        ],
        compiler_params=pltpu.CompilerParams(collective_id=1, has_side_effects=True),
    )(packed(block_output, [block_peak, block_mass]))
    centre_every = centre_every.reshape(heads_n * head_count, CLUSTERS, HDIM)

    ids_every = ids_every.reshape(heads_n * head_count, token_rows)
    member_every = (ids_every[:, None, :] == labels[None, :, None]).astype(jnp.bfloat16)
    attended_all = jnp.einsum(
        "hct,hcd->thd", member_every, centre_every, preferred_element_type=jnp.float32
    )
    attended_all = attended_all.astype(jnp.bfloat16).reshape(token_rows, -1)
    group_rows = attended_all.shape[1] // heads_n
    summed = jnp.zeros((token_rows, column_weight.shape[1]), jnp.float32)
    for group in range(heads_n):
        term = jnp.dot(
            attended_all[:, group * group_rows : (group + 1) * group_rows],
            column_weight[group * group_rows : (group + 1) * group_rows, :],
            preferred_element_type=jnp.float32,
        )
        summed = summed + term.astype(jnp.bfloat16).astype(jnp.float32)
    return summed.astype(jnp.bfloat16)


def solution(mesh):
    return jax.shard_map(
        local,
        mesh=mesh,
        in_specs=(
            P("seq", "head"),
            P("seq", "head"),
            P("seq", "head"),
            P("seq", "head"),
            P("head", "seq"),
        ),
        out_specs=P("seq", "head"),
        check_vma=False,
    )
```

time: 315 us -> 256 us (0.81)
  waiting for transfers between devices: 61.6 us -> 0.02 us
  Pallas kernels: 133 us -> 165 us
  blocking collectives: 30.6 us -> 0 us
    all_gather x2 -> x1, waiting for transfers between devices: 60.8 us -> 0.01 us  [local(): lax.all_gather(tall.reshape(-1, out_weight.shape[1]), 'seq', axis=1, tile...]
    pallas_call x2, Pallas kernels: 133 us -> 165 us  [the longest x1 89.3 us: local(): pl.pallas_call(functools.partial(centre_kernel, bits, heads_n, rows), out...]
    all_to_all x1 -> x0, blocking collectives: 30.6 us -> none  [local(): tall = lax.all_to_all(wide, 'head', split_axis=0, concat_axis=0, tiled=True)]
  transfers between devices with their start and end apart: 2 -> 1, of which waited for: 1 -> 0; matrix products, arithmetic and copies ran while one was open for 16% -> 17% of each run, Pallas kernels for 42% -> 29%
where the time goes in v2:
time: 256 us; the launch traced here: 255 us
  Pallas kernels  165 us (64%)
  matrix products  63.5 us (25%)
  other arithmetic  13.6 us (5%)
  between operations  13.5 us (5%)
    pallas_call x1, Pallas kernels, local(): pl.pallas_call(functools.partial(centre_kernel, bits, heads_n, rows), out...  89.3 us
    pallas_call x1, Pallas kernels, local(): pl.pallas_call(functools.partial(output_kernel, bits, heads_n, rows), out...  75.3 us
    dot_general x2, matrix products, local(): jnp.dot(attended_all[:, group * group_rows:(group + 1) * group_rows], col...  25.5 us
    dot_general x1, matrix products, local(): jnp.einsum('hcd,thd->hct', centre, key_three, preferred_element_type=jnp....  12.6 us
    dot_general x1, matrix products, local(): jnp.einsum('hct,hcd->thd', member_every, centre_every, preferred_element_...  11 us
    dot_general x1, matrix products, local(): jnp.einsum('hct,thd->hcd', weights, value_three, preferred_element_type=j...  9.26 us
    reduce_sum x1, other arithmetic, local(): block_mass = jnp.sum(weights, axis=2, dtype=jnp.float32)  7.91 us
    dot_general x1, matrix products, local(): jnp.einsum('hct,thd->hcd', member, query_three, preferred_element_type=jn...  5.17 us
  transfers between devices with their start and end apart: 1, of which 0 were waited for; matrix products, arithmetic and copies ran while one was open for 17% of the time, Pallas kernels for 29%

profile of v2, /device:TPU:0, one launch (start us, length us, event | category | flops | bytes accessed | tf_op | source)
XLA Modules:
  0.0 255.4 jit_solution(17888716883377049357)
XLA Ops:
  6.5 0.0 all-gather.2.cloned.1.call-start
  6.5 2.7 %convert_reduce_fusion.1 = f32[16,256]{1,0:T(8,128)S(1)} fusion(s32[16,1024]{1,0:T(8,128)} %bitcast.40), kind=kLoop, calls=%fused_computation.5 | loop fusion | flops 16773120 | bytes 81920 | tf_op jit(solution)/shard_map/reduce_sum | solution.py:271
  9.2 5.2 %fusion.3 = f32[16,256,128]{2,1,0:T(8,128)S(1)} fusion(s32[16,1024]{1,0:T(8,128)} %bitcast.41, bf16[1024,2048]{1,0:T(8,128)(2,1)} %param.5), kind=kOutput, calls=%fused_computation.8 | convolution fusion | flops 1077936128 | bytes 6356992 | tf_op jit(solution)/shard_map/hct,thd->hcd/dot_general | solution.py:270
  14.4 1.5 select_maximum_fusion.2.part_ref
  15.9 89.3 %shard_map.55 = (bf16[2,16,128,128]{3,2,1,0:T(8,128)(2,1)}, s32[2,16,1024]{2,1,0:T(8,128)}, bf16[2,2048,256]{2,1,0:T(8,128)(2,1)}) custom-call(f32[2,16,136,128]{3,2,1,0:T(8,128)} %select_maximum_fusion.2.part_ref, s32[16,1024]{1,0:T(8,128)} %bitcast.42, bf16[2048,256]{1,0:T(8,128)(2,1)} %weight_ref.1), custom_call_target="tpu_custom_call" | custom-call | tf_op jit(solution)/shard_map/pallas_call | solution.py:291
  105.3 0.0 all-gather.2.cloned.1.call-update
  105.3 12.6 %multiply_reduce_fusion = (f32[16,256]{1,0:T(8,128)S(1)}, f32[16,256,1024]{2,1,0:T(8,128)}) fusion(bf16[16,256,128]{2,1,0:T(8,128)(2,1)} %bitcast.39, bf16[1024,2048]{1,0:T(8,128)(2,1)} %param.6), kind=kOutput, calls=%fused_computation.9 | convolution fusion | flops 1082126336 | bytes 22036480 | tf_op jit(solution)/shard_map/hcd,thd->hct/dot_general | solution.py:320
  117.9 7.9 %convert_reduce_fusion = f32[16,256]{1,0:T(8,128)S(1)} fusion(f32[16,256]{1,0:T(8,128)S(1)} %get-tuple-element.11, f32[16,256,1024]{2,1,0:T(8,128)} %get-tuple-element.12), kind=kLoop, calls=%fused_computation.3 | loop fusion | flops 20967424 | bytes 16809984 | tf_op jit(solution)/shard_map/reduce_sum | solution.py:324
  125.8 9.3 %fusion.10 = f32[16,256,128]{2,1,0:T(8,128)S(1)} fusion(f32[16,256,1024]{2,1,0:T(8,128)} %get-tuple-element.12, f32[16,256]{1,0:T(8,128)S(1)} %get-tuple-element.11, bf16[1024,2048]{1,0:T(8,128)(2,1)} %param.7), kind=kOutput, calls=%fused_computation.17 | convolution fusion | flops 1086324736 | bytes 23085056 | tf_op jit(solution)/shard_map/hct,thd->hcd/dot_general | solution.py:325
  135.1 0.0 copy-start.1
  135.1 1.5 select_maximum_fusion.part_ref
  136.7 75.3 %shard_map.56 = bf16[2,2,16,128,128]{4,3,2,1,0:T(8,128)(2,1)} custom-call(f32[2,16,136,128]{3,2,1,0:T(8,128)} %select_maximum_fusion.part_ref), custom_call_target="tpu_custom_call" | custom-call | tf_op jit(solution)/shard_map/pallas_call | solution.py:329
  212.0 0.0 copy-done.1
  212.0 11.0 %fusion.9 = bf16[32,128,1024]{2,1,0:T(8,128)(2,1)} fusion(bf16[32,256,128]{2,1,0:T(8,128)(2,1)} %bitcast.37, s32[32,1024]{1,0:T(8,128)S(1)} %bitcast.43), kind=kOutput, calls=%fused_computation.16 | convolution fusion | flops 2160066560 | bytes 10616832 | tf_op jit(solution)/shard_map/hct,hcd->thd/dot_general | solution.py:347
  223.0 0.0 all-gather.2.cloned.1.call-done
  223.0 0.0 copy-start
  223.0 12.8 %fusion.4 = bf16[1024,2048]{1,0:T(8,128)(2,1)S(1)} fusion(bf16[4096,2048]{1,0:T(8,128)(2,1)} %all-gather.2.cloned.1.call-done, bf16[1024,4096]{0,1:T(8,128)(2,1)} %bitcast.44), kind=kOutput, calls=%fused_computation.10 | convolution fusion | flops 8589934592 | bytes 16777216 | tf_op jit(solution)/shard_map/dot_general | solution.py:354
  235.9 0.0 copy-done
  235.9 12.7 %add_convert_fusion = bf16[1024,2048]{1,0:T(8,128)(2,1)} fusion(bf16[1024,2048]{1,0:T(8,128)(2,1)S(1)} %fusion.4, bf16[4096,2048]{1,0:T(8,128)(2,1)S(1)} %copy-done, bf16[1024,4096]{0,1:T(8,128)(2,1)} %bitcast.45), kind=kOutput, calls=%fused_computation.14 | convolution fusion | flops 8600420352 | bytes 20971520 | tf_op jit(solution)/shard_map/dot_general | solution.py:354
  (3 shorter events, 0.1 us)
Async XLA Ops:
  6.5 216.5 %all-gather.2.cloned.1.call-start = ((), (), s32[]{:S(2)}) async-start(), calls=%async_computation | async-start | bytes 18874368 | tf_op jit(solution)/shard_map/all_gather | solution.py:314
  135.1 76.9 %copy-start.1 = (s32[2,16,1024]{2,1,0:T(8,128)S(1)}, s32[2,16,1024]{2,1,0:T(8,128)}, u32[]{:S(2)}) copy-start(s32[2,16,1024]{2,1,0:T(8,128)} %get-tuple-element.9) | copy-start | bytes 393220
  223.0 12.8 %copy-start = (bf16[4096,2048]{1,0:T(8,128)(2,1)S(1)}, bf16[4096,2048]{1,0:T(8,128)(2,1)}, u32[]{:S(2)}) copy-start(bf16[4096,2048]{1,0:T(8,128)(2,1)} %all-gather.2.cloned.1.call-done) | copy-start | bytes 50331652
Sparse Core Ops, SparseCore 0:
  105.4 110.9 all-gather.1

commit v3 on v2

--- a/solution.py
+++ b/solution.py
@@ -11,6 +11,7 @@
 CLUSTERS = 256
 LANES = 128
 STAT = 8
+PIECES = 4
 MESH = pl.DeviceIdType.MESH
 
 
@@ -42,7 +43,7 @@
     pl.semaphore_wait(barrier, len(targets))
 
 
-def halve(seq, bits, acc, recvs, send_sem, recv_sem, merge):
+def halve(seq, bits, acc, recvs, send_sem, recv_sem, merge, beside=None):
     n = 1 << bits
     orders = orders_of(bits)
     starts = [[jnp.int32(0)] for _ in orders]
@@ -77,10 +78,12 @@
             lax.fori_loop(0, n >> (step + 1), body, 0)
             if step + 1 < bits:
                 pending[stream] = begin(stream, step + 1)
+        if beside is not None:
+            beside(step)
     return starts
 
 
-def double(seq, bits, starts, views, send_sem, recv_sem):
+def double(seq, bits, starts, views, send_sem, recv_sem, beside=None):
     n = 1 << bits
     orders = orders_of(bits)
 
@@ -110,6 +113,8 @@
                 copy.wait()
             if step > 0:
                 pending[stream] = begin(stream, step - 1)
+        if beside is not None and step > 0:
+            beside(2 * bits - 1 - step)
 
 
 def centre_kernel(
@@ -137,33 +142,75 @@
         return pltpu.make_async_remote_copy(
             src_ref=src,
             dst_ref=dst,
-            send_sem=sends.at[step - 1],
-            recv_sem=receives.at[step - 1],
+            send_sem=sends(step - 1),
+            recv_sem=receives(step - 1),
             device_id={"head": lax.rem(head + step, heads_n)},
             device_id_type=MESH,
         )
 
-    load.wait()
-    across = []
-    for step in range(1, heads_n):
-        across.append(
+    height = weight_ref.shape[0] // PIECES
+
+    def across(piece):
+        span = pl.ds(piece * height, height)
+        return [
             pltpu.make_async_remote_copy(
-                src_ref=weight_ref,
-                dst_ref=wide.at[group],
-                send_sem=zsend.at[step - 1],
-                recv_sem=zrecv.at[step - 1],
+                src_ref=weight_ref.at[span],
+                dst_ref=wide.at[group, span],
+                send_sem=zsend.at[step - 1, piece],
+                recv_sem=zrecv.at[step - 1, piece],
                 device_id={"seq": lax.rem(seq + step * low, n)},
                 device_id_type=MESH,
             )
-        )
-    id_copies = [to_head(step, ids_ref, ids_all.at[head], isend, irecv) for step in range(1, heads_n)]
-    for copy in across + id_copies:
+            for step in range(1, heads_n)
+        ]
+
+    def sideways(piece):
+        span = pl.ds(piece * height, height)
+        return [
+            to_head(
+                step,
+                wide.at[lax.rem(head + step, heads_n), span],
+                tall.at[head, span],
+                lambda i: ysend.at[i, piece],
+                lambda i: yrecv.at[i, piece],
+            )
+            for step in range(1, heads_n)
+        ]
+
+    far = [across(piece) for piece in range(PIECES)]
+    near = [sideways(piece) for piece in range(PIECES)]
+    sent, passed = [], []
+
+    def send_piece():
+        if len(sent) < PIECES:
+            sent.append(True)
+            for copy in far[len(sent) - 1]:
+                copy.start()
+
+    def pass_piece():
+        if len(passed) < PIECES:
+            passed.append(True)
+            for copy in far[len(passed) - 1]:
+                copy.wait()
+            for copy in near[len(passed) - 1]:
+                copy.start()
+
+    def beside(step):
+        send_piece()
+        if step >= 2:
+            pass_piece()
+
+    send_piece()
+    id_copies = [to_head(step, ids_ref, ids_all.at[head], lambda i: isend.at[i], lambda i: irecv.at[i]) for step in range(1, heads_n)]
+    for copy in id_copies:
         copy.start()
+    load.wait()
+    own_weight.wait()
 
     def merge(stream, chunk, recv, i):
         acc[stream, chunk] = acc[stream, chunk] + recv[stream, i]
 
-    starts = halve(seq, bits, acc, recvs, send_sem, recv_sem, merge)
+    starts = halve(seq, bits, acc, recvs, send_sem, recv_sem, merge, beside)
     block = min(rows, LANES)
     for stream in range(2):
         mine = starts[stream][-1]
@@ -171,22 +218,20 @@
             span = slice(b * block, (b + 1) * block)
             count = columns_of(acc[stream, mine, rows + b : rows + b + 1, :])[:block]
             full[stream, mine, span, :] = (acc[stream, mine, span, :] / count).astype(jnp.bfloat16)
-    own_weight.wait()
-    for copy in across:
-        copy.wait()
-    beside = [to_head(s, wide.at[lax.rem(head + s, heads_n)], tall.at[head], ysend, yrecv) for s in range(1, heads_n)]
-    for copy in beside:
-        copy.start()
+    double(seq, bits, starts, [full], gsend, grecv, beside)
+    while len(passed) < PIECES:
+        send_piece()
+        pass_piece()
     puts = [pltpu.make_async_copy(wide.at[head], tall_ref.at[head], put_sem.at[0])]
     puts[0].start()
-    double(seq, bits, starts, [full], gsend, grecv)
     out_ref[...] = full[...]
     own.wait()
     for copy in id_copies:
         copy.wait()
     ids_out_ref[...] = ids_all[...]
-    for copy in beside:
-        copy.wait()
+    for copies in near:
+        for copy in copies:
+            copy.wait()
     for step in range(1, heads_n):
         other = lax.rem(head + step, heads_n)
         puts.append(pltpu.make_async_copy(tall.at[other], tall_ref.at[other], put_sem.at[step]))
@@ -252,6 +297,26 @@
     out_ref[...] = full[...]
 
 
+def attend_kernel(rows, centre_ref, key_ref, value_ref, out_ref):
+    scores = lax.dot_general(
+        centre_ref[0], key_ref[...], (((1,), (1,)), ((), ())), preferred_element_type=jnp.float32
+    )
+    scores = scores * (1.0 / HDIM**0.5)
+    peak = jnp.max(scores, axis=1, keepdims=True)
+    weights = jnp.exp(scores - peak).astype(jnp.bfloat16)
+    mass = jnp.sum(weights.astype(jnp.float32), axis=1, keepdims=True)
+    part = jnp.dot(weights, value_ref[...], preferred_element_type=jnp.float32)
+    block = min(rows, LANES)
+    for chunk in range(CLUSTERS // rows):
+        out_ref[0, chunk, :rows, :] = part[chunk * rows : (chunk + 1) * rows]
+        out_ref[0, chunk, rows:, :] = jnp.zeros((STAT, LANES), jnp.float32)
+        for b in range(rows // block):
+            first = chunk * rows + b * block
+            for offset, stat in ((0, peak), (4, mass)):
+                column = jnp.concatenate([stat[first : first + block]] * (LANES // block), axis=0)
+                out_ref[0, chunk, rows + offset + b : rows + offset + b + 1, :] = columns_of(column)[:1]
+
+
 def local(queries, keys, values, cluster_ids, out_weight):
     n = lax.axis_size("seq")
     heads_n = lax.axis_size("head")
@@ -261,8 +326,6 @@
     rows = head_count * CLUSTERS // n // 2
     blocks = max(rows // LANES, 1)
     query_three = queries.reshape(token_rows, head_count, HDIM)
-    key_three = keys.reshape(token_rows, head_count, HDIM)
-    value_three = values.reshape(token_rows, head_count, HDIM)
     labels = jnp.arange(CLUSTERS, dtype=jnp.int32)
 
     ids_t = cluster_ids.T
@@ -305,7 +368,7 @@
             pltpu.VMEM((heads_n, *out_weight.shape), jnp.bfloat16),
             *recvs,
             dma((2, bits)), dma((2, bits)), dma((2, bits, 1)), dma((2, bits, 1)),
-            dma((others,)), dma((others,)), dma((others,)), dma((others,)), dma((others,)), dma((others,)),
+            dma((others,)), dma((others,)), *[dma((others, PIECES)) for _ in range(4)],
             dma((3,)), dma((heads_n,)),
         ],
         compiler_params=pltpu.CompilerParams(collective_id=0, has_side_effects=True),
@@ -317,14 +380,23 @@
     )
     centre = centre.reshape(head_count, CLUSTERS, HDIM)
 
-    scores = jnp.einsum("hcd,thd->hct", centre, key_three, preferred_element_type=jnp.float32)
-    scores = scores * (1.0 / HDIM**0.5)
-    block_peak = jnp.max(scores, axis=2)
-    weights = jnp.exp(scores - block_peak[:, :, None]).astype(jnp.bfloat16)
-    block_mass = jnp.sum(weights, axis=2, dtype=jnp.float32)
-    block_output = jnp.einsum(
-        "hct,thd->hcd", weights, value_three, preferred_element_type=jnp.float32
-    )
+    chunks = CLUSTERS // rows
+    parts = pl.pallas_call(
+        functools.partial(attend_kernel, rows),
+        out_shape=jax.ShapeDtypeStruct((head_count, chunks, rows + STAT, HDIM), jnp.float32),
+        grid=(head_count,),
+        in_specs=[
+            pl.BlockSpec((1, CLUSTERS, HDIM), lambda h: (h, 0, 0)),
+            pl.BlockSpec((token_rows, HDIM), lambda h: (0, h)),
+            pl.BlockSpec((token_rows, HDIM), lambda h: (0, h)),
+        ],
+        out_specs=pl.BlockSpec((1, chunks, rows + STAT, HDIM), lambda h: (h, 0, 0, 0)),
+        cost_estimate=pl.CostEstimate(
+            flops=4 * head_count * CLUSTERS * token_rows * HDIM,
+            bytes_accessed=4 * head_count * token_rows * HDIM,
+            transcendentals=head_count * CLUSTERS * token_rows,
+        ),
+    )(centre, keys, values).reshape(2, n, rows + STAT, HDIM)
 
     centre_every = pl.pallas_call(
         functools.partial(output_kernel, bits, heads_n, rows),
@@ -339,7 +411,7 @@
             dma((2, others)), dma((2, others)), dma((1,)),
         ],
         compiler_params=pltpu.CompilerParams(collective_id=1, has_side_effects=True),
-    )(packed(block_output, [block_peak, block_mass]))
+    )(parts)
     centre_every = centre_every.reshape(heads_n * head_count, CLUSTERS, HDIM)
 
     ids_every = ids_every.reshape(heads_n * head_count, token_rows)

time: 256 us -> 237 us (0.926)
  matrix products: 63.5 us -> 41.7 us
  other arithmetic: 13.6 us -> 4.19 us
  Pallas kernels: 165 us -> 171 us
  waiting for transfers between devices: 0.02 us -> 5.95 us
    dot_general x2 -> x0, matrix products: 21.8 us -> none  [the longest x1 12.6 us: local(): jnp.einsum('hcd,thd->hct', centre, key_three, preferred_element_type=jnp....]
    pallas_call x0 -> x1, Pallas kernels: none -> 16.6 us  [local(): pl.pallas_call(functools.partial(attend_kernel, rows), out_shape=jax.Shap...]
    pallas_call x1, Pallas kernels: 89.3 us -> 77.7 us  [local(): pl.pallas_call(functools.partial(centre_kernel, bits, heads_n, rows), out...]
    reduce_sum x1 -> x0, other arithmetic: 7.91 us -> none  [local(): block_mass = jnp.sum(weights, axis=2, dtype=jnp.float32)]
    all_gather x1, waiting for transfers between devices: 0.01 us -> 5.93 us  [local(): lax.all_gather(tall.reshape(-1, out_weight.shape[1]), 'seq', axis=1, tile...]
  transfers between devices with their start and end apart: 1 -> 1, of which waited for: 0 -> 1; matrix products, arithmetic and copies ran while one was open for 17% -> 5% of each run, Pallas kernels for 29% -> 39%
where the time goes in v3:
time: 237 us; the launch traced here: 236 us
  Pallas kernels  171 us (72%)
  matrix products  41.7 us (18%)
  between operations  13.4 us (6%)
  waiting for transfers between devices  5.95 us (3%)
  other arithmetic  4.19 us (2%)
    pallas_call x1, Pallas kernels, local(): pl.pallas_call(functools.partial(centre_kernel, bits, heads_n, rows), out...  77.7 us
    pallas_call x1, Pallas kernels, local(): pl.pallas_call(functools.partial(output_kernel, bits, heads_n, rows), out...  76.7 us
    dot_general x2, matrix products, local(): jnp.dot(attended_all[:, group * group_rows:(group + 1) * group_rows], col...  25.7 us
    pallas_call x1, Pallas kernels, local(): pl.pallas_call(functools.partial(attend_kernel, rows), out_shape=jax.Shap...  16.6 us
    dot_general x1, matrix products, local(): jnp.einsum('hct,hcd->thd', member_every, centre_every, preferred_element_...  10.8 us
    all_gather x1, waiting for transfers between devices, local(): lax.all_gather(tall.reshape(-1, out_weight.shape[1]), 'seq', axis=1, tile...  5.93 us
    dot_general x1, matrix products, local(): jnp.einsum('hct,thd->hcd', member, query_three, preferred_element_type=jn...  5.17 us
  transfers between devices with their start and end apart: 1, of which 1 were waited for; matrix products, arithmetic and copies ran while one was open for 5% of the time, Pallas kernels for 39%

profile of v3, /device:TPU:0, one launch (start us, length us, event | category | flops | bytes accessed | tf_op | source)
XLA Modules:
  0.0 236.4 jit_solution(3371012663457973314)
XLA Ops:
  6.5 0.0 all-gather.2.cloned.1.call-start
  6.5 2.7 %convert_reduce_fusion = f32[16,256]{1,0:T(8,128)S(1)} fusion(s32[16,1024]{1,0:T(8,128)} %bitcast.23), kind=kLoop, calls=%fused_computation.3 | loop fusion | flops 16773120 | bytes 81920 | tf_op jit(solution)/shard_map/reduce_sum | solution.py:334
  9.2 5.2 %fusion.3 = f32[16,256,128]{2,1,0:T(8,128)S(1)} fusion(s32[16,1024]{1,0:T(8,128)} %bitcast.24, bf16[1024,2048]{1,0:T(8,128)(2,1)} %param.5), kind=kOutput, calls=%fused_computation.6 | convolution fusion | flops 1077936128 | bytes 6356992 | tf_op jit(solution)/shard_map/hct,thd->hcd/dot_general | solution.py:333
  14.4 1.5 select_maximum_fusion.part_ref
  15.9 77.7 %shard_map.55 = (bf16[2,16,128,128]{3,2,1,0:T(8,128)(2,1)}, s32[2,16,1024]{2,1,0:T(8,128)}, bf16[2,2048,256]{2,1,0:T(8,128)(2,1)}) custom-call(f32[2,16,136,128]{3,2,1,0:T(8,128)} %select_maximum_fusion.part_ref, s32[16,1024]{1,0:T(8,128)} %bitcast.25, bf16[2048,256]{1,0:T(8,128)(2,1)} %weight_ref.1), custom_call_target="tpu_custom_call" | custom-call | tf_op jit(solution)/shard_map/pallas_call | solution.py:354
  93.7 0.0 all-gather.2.cloned.1.call-update
  93.7 16.6 %shard_map.56 = f32[16,2,136,128]{3,2,1,0:T(8,128)} custom-call(bf16[16,256,128]{2,1,0:T(8,128)(2,1)} %bitcast.22, bf16[1024,2048]{1,0:T(8,128)(2,1)} %key_ref.1, bf16[1024,2048]{1,0:T(8,128)(2,1)} %value_ref.1), custom_call_target="tpu_custom_call" | custom-call | flops 2147483648 | bytes 8388608 | tf_op jit(solution)/shard_map/pallas_call | solution.py:384
  110.3 0.0 copy-start.1
  110.3 76.7 %shard_map.57 = bf16[2,2,16,128,128]{4,3,2,1,0:T(8,128)(2,1)} custom-call(f32[2,16,136,128]{3,2,1,0:T(8,128)} %bitcast.18), custom_call_target="tpu_custom_call" | custom-call | tf_op jit(solution)/shard_map/pallas_call | solution.py:401
  187.0 0.0 copy-done.1
  187.0 10.8 %fusion.9 = bf16[32,128,1024]{2,1,0:T(8,128)(2,1)} fusion(bf16[32,256,128]{2,1,0:T(8,128)(2,1)} %bitcast.20, s32[32,1024]{1,0:T(8,128)S(1)} %bitcast.26), kind=kOutput, calls=%fused_computation.13 | convolution fusion | flops 2160066560 | bytes 10616832 | tf_op jit(solution)/shard_map/hct,hcd->thd/dot_general | solution.py:419
  197.8 5.9 %all-gather.2.cloned.1.call-done = bf16[4096,2048]{1,0:T(8,128)(2,1)} async-done(((bf16[4096,256]{1,0:T(8,128)(2,1)}), bf16[4096,2048]{1,0:T(8,128)(2,1)}) %all-gather.2.cloned.1.call-update) | async-done | bytes 16777232 | tf_op jit(solution)/shard_map/all_gather | solution.py:377
  203.8 0.0 copy-start
  203.8 12.8 %fusion.4 = bf16[1024,2048]{1,0:T(8,128)(2,1)S(1)} fusion(bf16[4096,2048]{1,0:T(8,128)(2,1)} %all-gather.2.cloned.1.call-done, bf16[1024,4096]{0,1:T(8,128)(2,1)} %bitcast.27), kind=kOutput, calls=%fused_computation.7 | convolution fusion | flops 8589934592 | bytes 16777216 | tf_op jit(solution)/shard_map/dot_general | solution.py:426
  216.6 0.0 copy-done
  216.6 12.9 %add_convert_fusion = bf16[1024,2048]{1,0:T(8,128)(2,1)} fusion(bf16[1024,2048]{1,0:T(8,128)(2,1)S(1)} %fusion.4, bf16[4096,2048]{1,0:T(8,128)(2,1)S(1)} %copy-done, bf16[1024,4096]{0,1:T(8,128)(2,1)} %bitcast.28), kind=kOutput, calls=%fused_computation.11 | convolution fusion | flops 8600420352 | bytes 20971520 | tf_op jit(solution)/shard_map/dot_general | solution.py:426
  (1 shorter events, 0.0 us)
Async XLA Ops:
  6.5 197.2 %all-gather.2.cloned.1.call-start = ((), (), s32[]{:S(2)}) async-start(), calls=%async_computation | async-start | bytes 18874368 | tf_op jit(solution)/shard_map/all_gather | solution.py:377
  110.3 76.7 %copy-start.1 = (s32[2,16,1024]{2,1,0:T(8,128)S(1)}, s32[2,16,1024]{2,1,0:T(8,128)}, u32[]{:S(2)}) copy-start(s32[2,16,1024]{2,1,0:T(8,128)} %get-tuple-element.9) | copy-start | bytes 393220
  203.8 12.8 %copy-start = (bf16[4096,2048]{1,0:T(8,128)(2,1)S(1)}, bf16[4096,2048]{1,0:T(8,128)(2,1)}, u32[]{:S(2)}) copy-start(bf16[4096,2048]{1,0:T(8,128)(2,1)} %all-gather.2.cloned.1.call-done) | copy-start | bytes 50331652
Sparse Core Ops, SparseCore 0:
  93.8 109.9 all-gather.1

commit v4 on v3

--- a/solution.py
+++ b/solution.py
@@ -43,7 +43,7 @@
     pl.semaphore_wait(barrier, len(targets))
 
 
-def halve(seq, bits, acc, recvs, send_sem, recv_sem, merge, beside=None):
+def halve(seq, bits, make, merge, beside=None):
     n = 1 << bits
     orders = orders_of(bits)
     starts = [[jnp.int32(0)] for _ in orders]
@@ -54,25 +54,20 @@
         start = starts[stream][step]
         give = start + (1 - digit) * half
         starts[stream].append(start + digit * half)
-        copy = pltpu.make_async_remote_copy(
-            src_ref=acc.at[stream, pl.ds(give, half)],
-            dst_ref=recvs[step].at[stream],
-            send_sem=send_sem.at[stream, step],
-            recv_sem=recv_sem.at[stream, step],
-            device_id={"seq": partner},
-            device_id_type=MESH,
-        )
-        copy.start()
-        return copy
+        copies = make(stream, step, give, half, partner)
+        for copy in copies:
+            copy.start()
+        return copies
 
     pending = [begin(stream, 0) for stream in range(len(orders))]
     for step in range(bits):
         for stream in range(len(orders)):
-            pending[stream].wait()
+            for copy in pending[stream]:
+                copy.wait()
             keep = starts[stream][step + 1]
 
             def body(i, carry, stream=stream, keep=keep, step=step):
-                merge(stream, keep + i, recvs[step], i)
+                merge(stream, step, keep + i, i)
                 return carry
 
             lax.fori_loop(0, n >> (step + 1), body, 0)
@@ -118,13 +113,12 @@
 
 
 def centre_kernel(
-    bits, heads_n, rows, part_ref, ids_ref, weight_ref, out_ref, ids_out_ref, tall_ref, *scratch
+    bits, heads_n, rows, part_ref, ids_ref, weight_ref, out_ref, ids_out_ref, *refs
 ):
+    tall_refs, scratch = refs[:heads_n], refs[heads_n:]
     acc, ids_all, full, wide, tall = scratch[:5]
     recvs = scratch[5 : 5 + bits]
-    send_sem, recv_sem, gsend, grecv, isend, irecv, zsend, zrecv, ysend, yrecv, local_sem, put_sem = scratch[
-        5 + bits :
-    ]
+    send_sem, recv_sem, gsend, grecv, isend, irecv, zsend, zrecv, ysend, yrecv, local_sem = scratch[5 + bits :]
     seq = lax.axis_index("seq")
     head = lax.axis_index("head")
     n = 1 << bits
@@ -207,10 +201,22 @@
     load.wait()
     own_weight.wait()
 
-    def merge(stream, chunk, recv, i):
-        acc[stream, chunk] = acc[stream, chunk] + recv[stream, i]
-
-    starts = halve(seq, bits, acc, recvs, send_sem, recv_sem, merge, beside)
+    def make(stream, step, give, half, partner):
+        return [
+            pltpu.make_async_remote_copy(
+                src_ref=acc.at[stream, pl.ds(give, half)],
+                dst_ref=recvs[step].at[stream],
+                send_sem=send_sem.at[stream, step],
+                recv_sem=recv_sem.at[stream, step],
+                device_id={"seq": partner},
+                device_id_type=MESH,
+            )
+        ]
+
+    def merge(stream, step, chunk, i):
+        acc[stream, chunk] = acc[stream, chunk] + recvs[step][stream, i]
+
+    starts = halve(seq, bits, make, merge, beside)
     block = min(rows, LANES)
     for stream in range(2):
         mine = starts[stream][-1]
@@ -222,8 +228,6 @@
     while len(passed) < PIECES:
         send_piece()
         pass_piece()
-    puts = [pltpu.make_async_copy(wide.at[head], tall_ref.at[head], put_sem.at[0])]
-    puts[0].start()
     out_ref[...] = full[...]
     own.wait()
     for copy in id_copies:
@@ -232,18 +236,23 @@
     for copies in near:
         for copy in copies:
             copy.wait()
-    for step in range(1, heads_n):
-        other = lax.rem(head + step, heads_n)
-        puts.append(pltpu.make_async_copy(tall.at[other], tall_ref.at[other], put_sem.at[step]))
-        puts[-1].start()
-    for put in puts:
-        put.wait()
+    for index, ref in enumerate(tall_refs):
+
+        @pl.when(head == index)
+        def _(index=index, ref=ref):
+            ref[...] = wide[index]
+
+        @pl.when(head != index)
+        def _(index=index, ref=ref):
+            ref[...] = tall[index]
 
 
 def output_kernel(bits, heads_n, rows, part_ref, out_ref, *scratch):
     acc, full = scratch[:2]
-    recvs = scratch[2 : 2 + bits]
-    send_sem, recv_sem, gsend, grecv, hsend, hrecv, local_sem = scratch[2 + bits :]
+    outs = scratch[2 : 2 + bits]
+    recvs = scratch[2 + bits : 2 + 2 * bits]
+    stat_recvs = scratch[2 + 2 * bits : 2 + 3 * bits]
+    send_sem, recv_sem, gsend, grecv, hsend, hrecv, local_sem = scratch[2 + 3 * bits :]
     seq = lax.axis_index("seq")
     head = lax.axis_index("head")
     load = pltpu.make_async_copy(part_ref, acc, local_sem.at[0])
@@ -252,9 +261,32 @@
     load.wait()
     block = min(rows, LANES)
 
-    def merge(stream, chunk, recv, i):
+    def make(stream, step, give, half, partner):
+        def convert(i, carry):
+            outs[step][stream, i] = acc[stream, give + i, :rows, :].astype(jnp.bfloat16)
+            return carry
+
+        lax.fori_loop(0, half, convert, 0)
+        return [
+            pltpu.make_async_remote_copy(
+                src_ref=src,
+                dst_ref=dst,
+                send_sem=send_sem.at[stream, step, number],
+                recv_sem=recv_sem.at[stream, step, number],
+                device_id={"seq": partner},
+                device_id_type=MESH,
+            )
+            for number, (src, dst) in enumerate(
+                (
+                    (acc.at[stream, pl.ds(give, half), pl.ds(rows, STAT)], stat_recvs[step].at[stream]),
+                    (outs[step].at[stream], recvs[step].at[stream]),
+                )
+            )
+        ]
+
+    def merge(stream, step, chunk, i):
         mine = acc[stream, chunk, rows : rows + STAT, :]
-        other = recv[stream, i, rows : rows + STAT, :]
+        other = stat_recvs[step][stream, i]
         for b in range(rows // block):
             peak_a, peak_b = mine[b : b + 1], other[b : b + 1]
             peak = jnp.maximum(peak_a, peak_b)
@@ -266,10 +298,10 @@
             span = slice(b * block, (b + 1) * block)
             acc[stream, chunk, span, :] = (
                 acc[stream, chunk, span, :] * columns_of(scale_a)[:block]
-                + recv[stream, i, span, :] * columns_of(scale_b)[:block]
-            )
-
-    starts = halve(seq, bits, acc, recvs, send_sem, recv_sem, merge)
+                + recvs[step][stream, i, span, :].astype(jnp.float32) * columns_of(scale_b)[:block]
+            )
+
+    starts = halve(seq, bits, make, merge)
     copies = []
     for stream in range(2):
         mine = starts[stream][-1]
@@ -351,15 +383,15 @@
     dma = pltpu.SemaphoreType.DMA
     recvs = [pltpu.VMEM((2, n >> (bit + 1), rows + STAT, LANES), jnp.float32) for bit in range(bits)]
     others = max(heads_n - 1, 1)
-    centre, ids_every, tall = pl.pallas_call(
+    centre, ids_every, *tall = pl.pallas_call(
         functools.partial(centre_kernel, bits, heads_n, rows),
         out_shape=(
             jax.ShapeDtypeStruct((2, n, rows, HDIM), jnp.bfloat16),
             jax.ShapeDtypeStruct((heads_n, head_count, token_rows), jnp.int32),
-            jax.ShapeDtypeStruct((heads_n, *out_weight.shape), jnp.bfloat16),
+            *[jax.ShapeDtypeStruct(out_weight.shape, jnp.bfloat16) for _ in range(heads_n)],
         ),
         in_specs=[anywhere, vmem, anywhere],
-        out_specs=(vmem, vmem, anywhere),
+        out_specs=(vmem, vmem, *[vmem] * heads_n),
         scratch_shapes=[
             pltpu.VMEM((2, n, rows + STAT, LANES), jnp.float32),
             pltpu.VMEM((heads_n, head_count, token_rows), jnp.int32),
@@ -369,15 +401,16 @@
             *recvs,
             dma((2, bits)), dma((2, bits)), dma((2, bits, 1)), dma((2, bits, 1)),
             dma((others,)), dma((others,)), *[dma((others, PIECES)) for _ in range(4)],
-            dma((3,)), dma((heads_n,)),
+            dma((3,)),
         ],
         compiler_params=pltpu.CompilerParams(collective_id=0, has_side_effects=True),
     )(packed(totals, [counts]), ids_t, out_weight)
     low = n // heads_n
-    column_weight = lax.all_gather(
-        tall.reshape(-1, out_weight.shape[1]), "seq", axis=1, tiled=True,
-        axis_index_groups=[[g * low + r for r in range(low)] for g in range(heads_n)],
-    )
+    groups = [[g * low + r for r in range(low)] for g in range(heads_n)]
+    column_weight = [
+        lax.all_gather(tall[group], "seq", axis=1, tiled=True, axis_index_groups=groups)
+        for group in range(heads_n)
+    ]
     centre = centre.reshape(head_count, CLUSTERS, HDIM)
 
     chunks = CLUSTERS // rows
@@ -406,8 +439,9 @@
         scratch_shapes=[
             pltpu.VMEM((2, n, rows + STAT, LANES), jnp.float32),
             pltpu.VMEM((heads_n, 2, n, rows, HDIM), jnp.bfloat16),
-            *recvs,
-            dma((2, bits)), dma((2, bits)), dma((2, bits, heads_n)), dma((2, bits, heads_n)),
+            *[pltpu.VMEM((2, n >> (bit + 1), rows, LANES), jnp.bfloat16) for _ in range(2) for bit in range(bits)],
+            *[pltpu.VMEM((2, n >> (bit + 1), STAT, LANES), jnp.float32) for bit in range(bits)],
+            dma((2, bits, 2)), dma((2, bits, 2)), dma((2, bits, heads_n)), dma((2, bits, heads_n)),
             dma((2, others)), dma((2, others)), dma((1,)),
         ],
         compiler_params=pltpu.CompilerParams(collective_id=1, has_side_effects=True),
@@ -421,11 +455,11 @@
     )
     attended_all = attended_all.astype(jnp.bfloat16).reshape(token_rows, -1)
     group_rows = attended_all.shape[1] // heads_n
-    summed = jnp.zeros((token_rows, column_weight.shape[1]), jnp.float32)
+    summed = jnp.zeros((token_rows, column_weight[0].shape[1]), jnp.float32)
     for group in range(heads_n):
         term = jnp.dot(
             attended_all[:, group * group_rows : (group + 1) * group_rows],
-            column_weight[group * group_rows : (group + 1) * group_rows, :],
+            column_weight[group],
             preferred_element_type=jnp.float32,
         )
         summed = summed + term.astype(jnp.bfloat16).astype(jnp.float32)

time: 237 us -> 234 us (0.987)
  Pallas kernels: 171 us -> 149 us
  waiting for transfers between devices: 5.95 us -> 20.7 us
  matrix products: 41.7 us -> 45.3 us
    pallas_call x1, Pallas kernels: 76.7 us -> 55 us  [local(): pl.pallas_call(functools.partial(output_kernel, bits, heads_n, rows), out...]
    all_gather x1 -> x2, waiting for transfers between devices: 5.93 us -> 20.2 us  [local(): lax.all_gather(tall[group], 'seq', axis=1, tiled=True, axis_index_groups=...]
    dot_general x2, matrix products: 25.7 us -> 29.1 us  [local(): jnp.dot(attended_all[:, group * group_rows:(group + 1) * group_rows], col...]
  transfers between devices with their start and end apart: 1 -> 2, of which waited for: 1 -> 1; matrix products, arithmetic and copies ran while one was open for 5% -> 11% of each run, Pallas kernels for 39% -> 31%
where the time goes in v4:
time: 234 us; the launch traced here: 233 us
  Pallas kernels  149 us (64%)
  matrix products  45.3 us (19%)
  waiting for transfers between devices  20.7 us (9%)
  between operations  13.4 us (6%)
  other arithmetic  4.19 us (2%)
    pallas_call x1, Pallas kernels, local(): pl.pallas_call(functools.partial(centre_kernel, bits, heads_n, rows), out...  77.6 us
    pallas_call x1, Pallas kernels, local(): pl.pallas_call(functools.partial(output_kernel, bits, heads_n, rows), out...  55 us
    dot_general x2, matrix products, local(): jnp.dot(attended_all[:, group * group_rows:(group + 1) * group_rows], col...  29.1 us
    all_gather x2, waiting for transfers between devices, local(): lax.all_gather(tall[group], 'seq', axis=1, tiled=True, axis_index_groups=...  20.2 us
    pallas_call x1, Pallas kernels, local(): pl.pallas_call(functools.partial(attend_kernel, rows), out_shape=jax.Shap...  16.5 us
    dot_general x1, matrix products, local(): jnp.einsum('hct,hcd->thd', member_every, centre_every, preferred_element_...  11 us
    dot_general x1, matrix products, local(): jnp.einsum('hct,thd->hcd', member, query_three, preferred_element_type=jn...  5.17 us
  transfers between devices with their start and end apart: 2, of which 1 were waited for; matrix products, arithmetic and copies ran while one was open for 11% of the time, Pallas kernels for 31%

profile of v4, /device:TPU:0, one launch (start us, length us, event | category | flops | bytes accessed | tf_op | source)
XLA Modules:
  0.0 233.0 jit_solution(4056063511255986809)
XLA Ops:
  6.5 0.0 all-gather.5.cloned.1.call-start
  6.5 2.7 %convert_reduce_fusion = f32[16,256]{1,0:T(8,128)S(1)} fusion(s32[16,1024]{1,0:T(8,128)} %bitcast.23), kind=kLoop, calls=%fused_computation.3 | loop fusion | flops 16773120 | bytes 81920 | tf_op jit(solution)/shard_map/reduce_sum | solution.py:366
  9.2 5.2 %fusion.3 = f32[16,256,128]{2,1,0:T(8,128)S(1)} fusion(s32[16,1024]{1,0:T(8,128)} %bitcast.24, bf16[1024,2048]{1,0:T(8,128)(2,1)} %param.5), kind=kOutput, calls=%fused_computation.6 | convolution fusion | flops 1077936128 | bytes 6356992 | tf_op jit(solution)/shard_map/hct,thd->hcd/dot_general | solution.py:365
  14.4 1.5 select_maximum_fusion.part_ref
  15.9 77.6 %shard_map.55 = (bf16[2,16,128,128]{3,2,1,0:T(8,128)(2,1)}, s32[2,16,1024]{2,1,0:T(8,128)}, bf16[2048,256]{1,0:T(8,128)(2,1)}, bf16[2048,256]{1,0:T(8,128)(2,1)}) custom-call(f32[2,16,136,128]{3,2,1,0:T(8,128)} %select_maximum_fusion.part_ref, s32[16,1024]{1,0:T(8,128)} %bitcast.25, bf16[2048,256]{1,0:T(8,128)(2,1)} %weight_ref.1), custom_call_target="tpu_custom_call" | custom-call | tf_op jit(solution)/shard_map/pallas_call | solution.py:386
  93.5 0.0 all-gather.5.cloned.1.call-update
  93.5 0.2 all-gather.3.cloned.1.call-start
  93.8 0.5 all-gather.3.cloned.1.call-update
  94.3 16.5 %shard_map.56 = f32[16,2,136,128]{3,2,1,0:T(8,128)} custom-call(bf16[16,256,128]{2,1,0:T(8,128)(2,1)} %bitcast.22, bf16[1024,2048]{1,0:T(8,128)(2,1)} %key_ref.1, bf16[1024,2048]{1,0:T(8,128)(2,1)} %value_ref.1), custom_call_target="tpu_custom_call" | custom-call | flops 2147483648 | bytes 8388608 | tf_op jit(solution)/shard_map/pallas_call | solution.py:417
  110.8 0.0 copy-start
  110.8 55.0 %shard_map.57 = bf16[2,2,16,128,128]{4,3,2,1,0:T(8,128)(2,1)} custom-call(f32[2,16,136,128]{3,2,1,0:T(8,128)} %bitcast.19), custom_call_target="tpu_custom_call" | custom-call | tf_op jit(solution)/shard_map/pallas_call | solution.py:434
  165.8 0.0 copy-done
  165.8 11.0 %fusion.5 = bf16[32,128,1024]{2,1,0:T(8,128)(2,1)} fusion(bf16[32,256,128]{2,1,0:T(8,128)(2,1)} %bitcast.20, s32[32,1024]{1,0:T(8,128)S(1)} %bitcast.26), kind=kOutput, calls=%fused_computation.9 | convolution fusion | flops 2160066560 | bytes 10616832 | tf_op jit(solution)/shard_map/hct,hcd->thd/dot_general | solution.py:453
  176.8 0.0 all-gather.5.cloned.1.call-done
  176.8 14.0 %fusion.8 = bf16[1024,2048]{1,0:T(8,128)(2,1)} fusion(bf16[2048,2048]{1,0:T(8,128)(2,1)} %all-gather.5.cloned.1.call-done, bf16[1024,4096]{0,1:T(8,128)(2,1)} %bitcast.27), kind=kOutput, calls=%fused_computation.12 | convolution fusion | flops 8589934592 | bytes 16777216 | tf_op jit(solution)/shard_map/dot_general | solution.py:460
  190.8 20.2 %all-gather.3.cloned.1.call-done = bf16[2048,2048]{1,0:T(8,128)(2,1)} async-done(((bf16[2048,256]{1,0:T(8,128)(2,1)}), bf16[2048,2048]{1,0:T(8,128)(2,1)}) %all-gather.3.cloned.1.call-update) | async-done | bytes 8388624 | tf_op jit(solution)/shard_map/all_gather | solution.py:411
  211.0 15.1 %add_convert_fusion = bf16[1024,2048]{1,0:T(8,128)(2,1)} fusion(bf16[1024,2048]{1,0:T(8,128)(2,1)} %fusion.8, bf16[2048,2048]{1,0:T(8,128)(2,1)} %all-gather.3.cloned.1.call-done, bf16[1024,4096]{0,1:T(8,128)(2,1)} %bitcast.28), kind=kOutput, calls=%fused_computation.7 | convolution fusion | flops 8600420352 | bytes 20971520 | tf_op jit(solution)/shard_map/dot_general | solution.py:460
  (1 shorter events, 0.0 us)
Async XLA Ops:
  6.5 170.3 %all-gather.5.cloned.1.call-start = ((), (), s32[]{:S(2)}) async-start(), calls=%async_computation.1 | async-start | bytes 9437184 | tf_op jit(solution)/shard_map/all_gather | solution.py:411
  93.5 117.5 %all-gather.3.cloned.1.call-start = ((), (), s32[]{:S(2)}) async-start(), calls=%async_computation | async-start | bytes 9437184 | tf_op jit(solution)/shard_map/all_gather | solution.py:411
  110.8 55.0 %copy-start = (s32[2,16,1024]{2,1,0:T(8,128)S(1)}, s32[2,16,1024]{2,1,0:T(8,128)}, u32[]{:S(2)}) copy-start(s32[2,16,1024]{2,1,0:T(8,128)} %get-tuple-element.10) | copy-start | bytes 393220
Sparse Core Ops, SparseCore 0:
  93.6 63.8 all-gather.4
  159.1 51.8 all-gather.2

commit v5 on v4

--- a/solution.py
+++ b/solution.py
@@ -191,9 +191,10 @@
 
     def beside(step):
         send_piece()
-        if step >= 2:
+        if step >= 1:
             pass_piece()
 
+    send_piece()
     send_piece()
     id_copies = [to_head(step, ids_ref, ids_all.at[head], lambda i: isend.at[i], lambda i: irecv.at[i]) for step in range(1, heads_n)]
     for copy in id_copies:

time: 234 us -> 234 us (level)
  no operation moved by 1% of the time
where the time goes in v5:
time: 234 us
  Pallas kernels  148 us (63%)
  matrix products  45.1 us (19%)
  waiting for transfers between devices  22.7 us (10%)
  between operations  13.4 us (6%)
  other arithmetic  4.19 us (2%)
    pallas_call x1, Pallas kernels, local(): pl.pallas_call(functools.partial(centre_kernel, bits, heads_n, rows), out...  76.7 us
    pallas_call x1, Pallas kernels, local(): pl.pallas_call(functools.partial(output_kernel, bits, heads_n, rows), out...  54.7 us
    dot_general x2, matrix products, local(): jnp.dot(attended_all[:, group * group_rows:(group + 1) * group_rows], col...  29.1 us
    all_gather x2, waiting for transfers between devices, local(): lax.all_gather(tall[group], 'seq', axis=1, tiled=True, axis_index_groups=...  22.2 us
    pallas_call x1, Pallas kernels, local(): pl.pallas_call(functools.partial(attend_kernel, rows), out_shape=jax.Shap...  16.6 us
    dot_general x1, matrix products, local(): jnp.einsum('hct,hcd->thd', member_every, centre_every, preferred_element_...  10.8 us
    dot_general x1, matrix products, local(): jnp.einsum('hct,thd->hcd', member, query_three, preferred_element_type=jn...  5.17 us
  transfers between devices with their start and end apart: 2, of which 1 were waited for; matrix products, arithmetic and copies ran while one was open for 11% of the time, Pallas kernels for 31%

profile of v5, /device:TPU:0, one launch (start us, length us, event | category | flops | bytes accessed | tf_op | source)
XLA Modules:
  0.0 233.7 jit_solution(15930625004467337733)
XLA Ops:
  6.5 0.0 all-gather.5.cloned.1.call-start
  6.5 2.7 %convert_reduce_fusion = f32[16,256]{1,0:T(8,128)S(1)} fusion(s32[16,1024]{1,0:T(8,128)} %bitcast.23), kind=kLoop, calls=%fused_computation.3 | loop fusion | flops 16773120 | bytes 81920 | tf_op jit(solution)/shard_map/reduce_sum | solution.py:367
  9.2 5.2 %fusion.3 = f32[16,256,128]{2,1,0:T(8,128)S(1)} fusion(s32[16,1024]{1,0:T(8,128)} %bitcast.24, bf16[1024,2048]{1,0:T(8,128)(2,1)} %param.5), kind=kOutput, calls=%fused_computation.6 | convolution fusion | flops 1077936128 | bytes 6356992 | tf_op jit(solution)/shard_map/hct,thd->hcd/dot_general | solution.py:366
  14.4 1.5 select_maximum_fusion.part_ref
  15.9 76.7 %shard_map.55 = (bf16[2,16,128,128]{3,2,1,0:T(8,128)(2,1)}, s32[2,16,1024]{2,1,0:T(8,128)}, bf16[2048,256]{1,0:T(8,128)(2,1)}, bf16[2048,256]{1,0:T(8,128)(2,1)}) custom-call(f32[2,16,136,128]{3,2,1,0:T(8,128)} %select_maximum_fusion.part_ref, s32[16,1024]{1,0:T(8,128)} %bitcast.25, bf16[2048,256]{1,0:T(8,128)(2,1)} %weight_ref.1), custom_call_target="tpu_custom_call" | custom-call | tf_op jit(solution)/shard_map/pallas_call | solution.py:387
  92.6 0.0 all-gather.5.cloned.1.call-update
  92.7 0.2 all-gather.3.cloned.1.call-start
  92.9 0.5 all-gather.3.cloned.1.call-update
  93.4 16.6 %shard_map.56 = f32[16,2,136,128]{3,2,1,0:T(8,128)} custom-call(bf16[16,256,128]{2,1,0:T(8,128)(2,1)} %bitcast.22, bf16[1024,2048]{1,0:T(8,128)(2,1)} %key_ref.1, bf16[1024,2048]{1,0:T(8,128)(2,1)} %value_ref.1), custom_call_target="tpu_custom_call" | custom-call | flops 2147483648 | bytes 8388608 | tf_op jit(solution)/shard_map/pallas_call | solution.py:418
  110.0 0.0 copy-start
  110.0 54.7 %shard_map.57 = bf16[2,2,16,128,128]{4,3,2,1,0:T(8,128)(2,1)} custom-call(f32[2,16,136,128]{3,2,1,0:T(8,128)} %bitcast.19), custom_call_target="tpu_custom_call" | custom-call | tf_op jit(solution)/shard_map/pallas_call | solution.py:435
  164.7 0.0 copy-done
  164.7 10.8 %fusion.5 = bf16[32,128,1024]{2,1,0:T(8,128)(2,1)} fusion(bf16[32,256,128]{2,1,0:T(8,128)(2,1)} %bitcast.20, s32[32,1024]{1,0:T(8,128)S(1)} %bitcast.26), kind=kOutput, calls=%fused_computation.9 | convolution fusion | flops 2160066560 | bytes 10616832 | tf_op jit(solution)/shard_map/hct,hcd->thd/dot_general | solution.py:454
  175.6 0.0 all-gather.5.cloned.1.call-done
  175.6 14.0 %fusion.8 = bf16[1024,2048]{1,0:T(8,128)(2,1)} fusion(bf16[2048,2048]{1,0:T(8,128)(2,1)} %all-gather.5.cloned.1.call-done, bf16[1024,4096]{0,1:T(8,128)(2,1)} %bitcast.27), kind=kOutput, calls=%fused_computation.12 | convolution fusion | flops 8589934592 | bytes 16777216 | tf_op jit(solution)/shard_map/dot_general | solution.py:461
  189.6 22.2 %all-gather.3.cloned.1.call-done = bf16[2048,2048]{1,0:T(8,128)(2,1)} async-done(((bf16[2048,256]{1,0:T(8,128)(2,1)}), bf16[2048,2048]{1,0:T(8,128)(2,1)}) %all-gather.3.cloned.1.call-update) | async-done | bytes 8388624 | tf_op jit(solution)/shard_map/all_gather | solution.py:412
  211.8 15.1 %add_convert_fusion = bf16[1024,2048]{1,0:T(8,128)(2,1)} fusion(bf16[1024,2048]{1,0:T(8,128)(2,1)} %fusion.8, bf16[2048,2048]{1,0:T(8,128)(2,1)} %all-gather.3.cloned.1.call-done, bf16[1024,4096]{0,1:T(8,128)(2,1)} %bitcast.28), kind=kOutput, calls=%fused_computation.7 | convolution fusion | flops 8600420352 | bytes 20971520 | tf_op jit(solution)/shard_map/dot_general | solution.py:461
  (1 shorter events, 0.0 us)
Async XLA Ops:
  6.5 169.0 %all-gather.5.cloned.1.call-start = ((), (), s32[]{:S(2)}) async-start(), calls=%async_computation.1 | async-start | bytes 9437184 | tf_op jit(solution)/shard_map/all_gather | solution.py:412
  92.7 119.1 %all-gather.3.cloned.1.call-start = ((), (), s32[]{:S(2)}) async-start(), calls=%async_computation | async-start | bytes 9437184 | tf_op jit(solution)/shard_map/all_gather | solution.py:412
  110.0 54.7 %copy-start = (s32[2,16,1024]{2,1,0:T(8,128)S(1)}, s32[2,16,1024]{2,1,0:T(8,128)}, u32[]{:S(2)}) copy-start(s32[2,16,1024]{2,1,0:T(8,128)} %get-tuple-element.10) | copy-start | bytes 393220
Sparse Core Ops, SparseCore 0:
  92.8 64.6 all-gather.4
  159.1 52.6 all-gather.2
